TPU v7x, 32 devices: a whole 2x2x4 slice. The times are simulated.
32 devices in a mesh: field: 2 (over y), sky: 4 (over z), epoch: 2 (over x), vel: 2 (over core).
Axes of the slice: x: 2, y: 2, z: 4, core: 2. Of those that a mesh axis runs over, the one named last changes fastest.
Arguments:
- images: bfloat16 [64, 8, 128, 128], P(('epoch', 'vel'), ('field', 'sky')), parts along dimension 1, may hold values from -6 to 6
- variances: bfloat16 [64, 8, 128, 128], P(('epoch', 'vel'), ('field', 'sky')), parts along dimension 1, may hold values from 0.5 to 2
- valid: int32 [64, 8], P(('epoch', 'vel'), ('field', 'sky')), parts along dimension 1, may hold values from 0 to 1, as said below
- psf_sigma: float32 [128], P(('field', 'epoch', 'vel')), parts along dimension 0, may hold values from 0.8 to 2.5
- offsets: int32 [2, 16, 64], P(None, None, 'epoch'), may hold values from -12 to 12, as said below
Outputs:
- likelihood: float32 [16, 8, 128, 128], P(('epoch', 'vel'), ('field', 'sky')), parts along dimension 1
- flux: float32 [16, 8, 128, 128], P(('epoch', 'vel'), ('field', 'sky')), parts along dimension 1
There are 2 independent parts, one for each index of `field`. A program takes and returns all parts, laid end to end along the dimension named above; an argument that names none is the same for every part. Nothing has to cross between parts.
Inputs may be any that keep to these rules, and one draw needn't show every extreme that they name: Each hypothesis moves linearly: offsets[c, k, e] = floor(s[c, k] * e / 63) for integer speeds s within the range; both ends of the range are reached. `valid`: in one tile of the field, drawn from the seed, exactly one epoch is usable; in every other tile each frame is usable with probability 3/4, independently.
All inputs are finite; a program needn't handle non-finite values.
Results may differ from a plain program's by a relative error of at most 0.0058.
Values may be sent and summed in bfloat16 or wider, within the bound.
A program may use at most 64 MiB of HBM per device.

v0:
```python
import functools

import jax
import jax.numpy as jnp
from jax import lax
from jax.experimental import pallas as pl
from jax.experimental.pallas import tpu as pltpu
from jax.sharding import PartitionSpec as P

VELS = 16
REACH = 12
PSFR = 7
GRID_X = 4
MARGIN = REACH + PSFR
LANES = 128

phi_floor = 0.25


def shifted(block, axis, distance):
    devices = range(lax.axis_size(axis))
    route = [((i - distance) % len(devices), i) for i in devices]
    return lax.ppermute(block, axis, route)


def positions(index, tile):
    return jnp.where(
        index < tile,
        index,
        jnp.where(
            index < tile + MARGIN,
            index - tile - MARGIN,
            jnp.where(index < tile + 2 * MARGIN, index - MARGIN, 4 * tile),
        ),
    )


FAR = -1.0e9


def exponents(distance):
    away = distance.astype(jnp.float32)
    return jnp.where(jnp.abs(distance) <= PSFR, -0.5 * away * away, FAR)


def fused_kernel(plan, *refs):
    tile, sky, blocks, block, epochs, runs, widths, exchange = plan
    if exchange:
        (offsets, motion, sigmas, valid, images, variances, psi_out, phi_out, plane_a, plane_b, ends, ends_made, ends_sem, row_q,
         own_q, side_q, bands, send_v, recv_v, send_x, recv_x, keep, sv, rv, sx, rx,
         own, building, sent_sides, came_sides, sz, rz) = refs
    else:
        (offsets, motion, sigmas, own, halo, psi_out, phi_out, plane_a, plane_b, ends, ends_made, ends_sem, row_q,
         own_q, side_q, bands, send_v, recv_v, send_x, recv_x, keep, sv, rv, sx, rx) = refs
    maps = 2
    rows_in = row_q.shape[1]
    rows_out = plane_a.shape[1]
    width = 2 * LANES
    mesh_id = pl.DeviceIdType.MESH
    me = lax.axis_index("sky")
    group = lax.axis_index("epoch")
    member = lax.axis_index("vel")
    column = lax.rem(lax.rem(me + GRID_X // 2, sky), GRID_X)
    before = lax.rem(me + sky - 1, sky)
    after = lax.rem(me + 1, sky)
    partner = 1 - member

    if exchange:
        wide, slots = widths[0]
        for at, (each_wide, each_slots) in enumerate(widths):
            here = 2 * group + member == at
            wide = jnp.where(here, each_wide, wide)
            slots = jnp.where(here, each_slots, slots)

    barrier = pltpu.get_barrier_semaphore()
    greeted = 1
    pl.semaphore_signal(barrier, inc=1, device_id={"vel": partner}, device_id_type=mesh_id)
    for a in range(1, blocks):
        peer = lax.rem(group + a, blocks)
        pl.semaphore_signal(barrier, inc=1, device_id={"epoch": peer}, device_id_type=mesh_id)
        greeted += 1
    if exchange:
        for other in (before, after):
            pl.semaphore_signal(barrier, inc=1, device_id={"sky": other}, device_id_type=mesh_id)
            greeted += 1

    if exchange:
        groups = sent_sides.shape[1]
        lane = lax.broadcasted_iota(jnp.int32, (tile, LANES), 1)

        def side_copy(to_after, g):
            return pltpu.make_async_remote_copy(
                src_ref=sent_sides.at[to_after, g],
                dst_ref=came_sides.at[to_after, g],
                send_sem=sz.at[to_after, g],
                recv_sem=rz.at[to_after, g],
                device_id={"sky": after if to_after else before},
                device_id_type=mesh_id,
            )

        building[...] = jnp.zeros_like(building)

        @pl.when(column == 0)
        def _():
            came_sides[1] = jnp.zeros_like(came_sides[1])

        @pl.when(column == GRID_X - 1)
        def _():
            came_sides[0] = jnp.zeros_like(came_sides[0])

        pl.semaphore_wait(barrier, greeted)

        def weigh(e, carry):
            s = lax.rem(e, slots)
            g = e // slots
            usable = valid[e].astype(jnp.float32)
            inverse = usable / variances[e, 0].astype(jnp.float32)
            scaled = images[e, 0].astype(jnp.float32) * inverse
            to_slot = wide * s
            to_mirror = wide * (slots - 1 - s)
            for m, field in enumerate((scaled, inverse)):
                own[e, m] = field.astype(jnp.bfloat16)
                low = pltpu.roll(field, to_mirror, axis=1)
                high = pltpu.roll(field, lax.rem(to_slot + wide, LANES), axis=1)
                at_low = (lane >= to_mirror) & (lane < to_mirror + wide)
                at_high = (lane >= to_slot) & (lane < to_slot + wide)
                building[0, m] = jnp.where(at_low, low, building[0, m])
                building[1, m] = jnp.where(at_high, high, building[1, m])

            @pl.when((s == slots - 1) | (e == epochs - 1))
            def _():
                sent_sides[0, g] = building[0].astype(jnp.bfloat16)
                sent_sides[1, g] = building[1].astype(jnp.bfloat16)

                @pl.when(column > 0)
                def _():
                    side_copy(0, g).start()

                @pl.when(column < GRID_X - 1)
                def _():
                    side_copy(1, g).start()

            return carry

        lax.fori_loop(0, epochs, weigh, 0)
    else:
        pl.semaphore_wait(barrier, greeted)

    shape = (rows_out, rows_in)
    row_q[...] = exponents(
        positions(lax.broadcasted_iota(jnp.int32, shape, 1), tile)
        - lax.broadcasted_iota(jnp.int32, shape, 0) + REACH
    )
    shape = (LANES, width)
    held = lax.broadcasted_iota(jnp.int32, shape, 0)
    shifted_out = lax.broadcasted_iota(jnp.int32, shape, 1) - REACH
    own_q[...] = exponents(held - shifted_out)
    if exchange:

        def place_strips(s, carry):
            low, high = wide * s, wide * (slots - 1 - s)
            pixel = jnp.where(
                (held >= low) & (held < low + wide),
                held - low - wide,
                jnp.where((held >= high) & (held < high + wide), held - high + tile, 4 * tile),
            )
            side_q[s] = exponents(pixel - shifted_out)
            return carry

        lax.fori_loop(0, slots, place_strips, 0)
    else:
        side_q[0] = exponents(positions(held + tile, tile) - shifted_out)

    first = member * epochs

    at_epoch = lax.broadcasted_iota(jnp.int32, motion.shape[1:], 1)
    moved = jnp.zeros(motion.shape[1:], jnp.int32)
    for way in range(2):
        start = jnp.where(at_epoch == first, motion[way], 0)
        moved += jnp.abs(motion[way] - jnp.sum(start, axis=1, keepdims=True))
    held_here = (at_epoch >= first) & (at_epoch < first + epochs)
    counted = jnp.zeros(ends_made.shape, jnp.int32)
    at_run = lax.broadcasted_iota(jnp.int32, ends_made.shape, 1)
    for run in range(runs - 1):
        count = jnp.sum((held_here & (moved <= run)).astype(jnp.int32), axis=1, keepdims=True)
        counted = jnp.where(at_run == run, count, counted)
    ends_made[...] = counted
    ends_copy = pltpu.make_async_copy(ends_made, ends, ends_sem)
    ends_copy.start()
    plane_a[:maps] = jnp.zeros_like(plane_a[:maps])
    plane_b[:maps] = jnp.zeros_like(plane_b[:maps])

    def correlate(e, turn):
        sigma = jnp.full((8, LANES), sigmas[e], jnp.float32)
        power = 1.0 / (sigma * sigma)
        tap = lax.broadcasted_iota(jnp.int32, (8, LANES), 1) - PSFR
        norm = jnp.sum(jnp.exp(exponents(tap) * power), axis=1, keepdims=True)
        scale = (1.0 / norm)[:1]
        power = power[:1, :1]

        def both(q):
            profile = jnp.exp(q * power) * scale
            return profile.astype(jnp.bfloat16), (profile * profile).astype(jnp.bfloat16)

        row_bands = both(row_q[...])
        s = lax.rem(e, slots) if exchange else 0
        for part, q in enumerate((own_q[...], side_q[s])):
            for m, made in enumerate(both(q)):
                bands[turn, m, part * LANES : (part + 1) * LANES] = made
        if exchange:
            g = e // slots
            lane = lax.broadcasted_iota(jnp.int32, (tile, LANES), 1)
            in_slot = (lane >= wide * s) & (lane < wide * s + wide)
        for m in range(maps):
            if exchange:
                side = jnp.where(
                    in_slot,
                    came_sides[1, g, m].astype(jnp.float32),
                    came_sides[0, g, m].astype(jnp.float32),
                ).astype(jnp.bfloat16)
            else:
                side = halo[e, m]
            held = jnp.concatenate([own[e, m], side], axis=1)
            rows = jnp.dot(row_bands[m], held, preferred_element_type=jnp.float32)
            done = jnp.dot(
                rows.astype(jnp.bfloat16), bands[turn, m], preferred_element_type=jnp.float32
            )
            at = maps * e + m
            plane_a[at + maps] = plane_a[at] + done[:, :LANES]
            plane_b[at + maps] = plane_b[at] + done[:, LANES:]

    step = 2 if epochs % 2 == 0 else 1

    def several(i, carry):
        for turn in range(step):
            correlate(step * i + turn, turn)
        return carry

    if exchange:
        for g in range(groups):

            @pl.when((column < GRID_X - 1) & (g * slots < epochs))
            def _():
                side_copy(0, g).wait_recv()

            @pl.when((column > 0) & (g * slots < epochs))
            def _():
                side_copy(1, g).wait_recv()

            begin = jnp.minimum(g * slots, epochs) // step
            end = jnp.minimum((g + 1) * slots, epochs) // step
            lax.fori_loop(begin, end, several, 0)
    else:
        lax.fori_loop(0, epochs // step, several, 0)

    def vel_copy(at):
        return pltpu.make_async_remote_copy(
            src_ref=send_v.at[at], dst_ref=recv_v.at[at], send_sem=sv.at[at], recv_sem=rv.at[at],
            device_id={"vel": partner}, device_id_type=mesh_id,
        )

    def epoch_copy(at):
        peer = lax.rem(group + 1 + at // block, blocks)
        return pltpu.make_async_remote_copy(
            src_ref=send_x.at[at], dst_ref=recv_x.at[at], send_sem=sx.at[at], recv_sem=rx.at[at],
            device_id={"epoch": peer}, device_id_type=mesh_id,
        )

    def stack(slot, carry):
        a = blocks - 1 - slot // (2 * block)
        turn = lax.rem(slot, 2 * block)
        mine = ((turn > 0) & (lax.rem(turn, 2) == 0)) | (turn == 2 * block - 1)
        b = jnp.where(mine, 0, 1)
        j = jnp.where(turn == 2 * block - 1, block - 1, jnp.where(mine, turn // 2 - 1, (turn + 1) // 2))
        place = a * block + j
        k = (lax.rem(group + a, blocks) * 2 + lax.rem(member + b, 2)) * block + j
        lane = lax.broadcasted_iota(jnp.int32, (tile, LANES), 1)
        summed = [jnp.zeros((tile, LANES), jnp.float32) for _ in range(maps)]
        low = jnp.zeros((), jnp.int32)
        for run in range(runs):
            high = ends[k, run] if run < runs - 1 else epochs
            at = first + jnp.minimum(low, epochs - 1)
            down = offsets[0, k, at] + REACH
            right = offsets[1, k, at] + REACH
            rows = pl.ds(down, tile)
            for m in range(maps):
                left_part = plane_a[maps * high + m, rows, :] - plane_a[maps * low + m, rows, :]
                right_part = plane_b[maps * high + m, rows, :] - plane_b[maps * low + m, rows, :]
                merged = jnp.where(lane >= right, left_part, right_part)
                summed[m] += pltpu.roll(merged, LANES - right, axis=1)
            low = high
        for m in range(maps):
            keep[b, j, m] = summed[m]

        @pl.when(b == 1)
        def _():
            send_v[place] = keep[1, j].astype(jnp.bfloat16)
            vel_copy(place).start()

        @pl.when(b == 0)
        def _():
            vel_copy(place).wait_recv()
            keep[0, j] = keep[0, j] + recv_v[place].astype(jnp.float32)

            @pl.when(a > 0)
            def _():
                send_x[place - block] = keep[0, j].astype(jnp.bfloat16)
                epoch_copy(place - block).start()

        return carry

    ends_copy.wait()
    lax.fori_loop(0, 2 * blocks * block, stack, 0)

    def finish(j, carry):
        total = keep[0, j]
        for a in range(1, blocks):
            at = (a - 1) * block + j
            epoch_copy(at).wait_recv()
            total = total + recv_x[at].astype(jnp.float32)
        psi_out[j] = total[0]
        phi_out[j] = total[1]
        return carry

    lax.fori_loop(0, block, finish, 0)

    def drain_v(at, carry):
        vel_copy(at).wait_send()
        return carry

    lax.fori_loop(0, blocks * block, drain_v, 0)

    def drain_x(at, carry):
        epoch_copy(at).wait_send()
        return carry

    lax.fori_loop(0, (blocks - 1) * block, drain_x, 0)
    if exchange:

        def drain_z(g, carry):
            @pl.when((column > 0) & (g * slots < epochs))
            def _():
                side_copy(0, g).wait_send()

            @pl.when((column < GRID_X - 1) & (g * slots < epochs))
            def _():
                side_copy(1, g).wait_send()

            return carry

        lax.fori_loop(0, groups, drain_z, 0)


def strips(own, tile_count, tile):
    position = (lax.axis_index("sky") + GRID_X // 2) % tile_count
    column = position % GRID_X
    left = shifted(own[..., tile - MARGIN :], "sky", 1)
    right = shifted(own[..., :MARGIN], "sky", -1)
    left = jnp.where(column > 0, left, jnp.zeros_like(left))
    right = jnp.where(column < GRID_X - 1, right, jnp.zeros_like(right))
    blank = jnp.zeros(own.shape[:3] + (LANES - 2 * MARGIN,), jnp.bfloat16)
    both = jnp.concatenate([own, left, right, blank], axis=3)
    upper = shifted(both[:, :, tile - MARGIN :], "sky", GRID_X)
    lower = shifted(both[:, :, :MARGIN], "sky", -GRID_X)
    upper = jnp.where(position >= GRID_X, upper, jnp.zeros_like(upper))
    lower = jnp.where(position < tile_count - GRID_X, lower, jnp.zeros_like(lower))
    blank = jnp.zeros(both.shape[:2] + (LANES - 2 * MARGIN, both.shape[3]), jnp.bfloat16)
    both = jnp.concatenate([both, upper, lower, blank], axis=2)
    return both[..., :tile], both[..., tile:]


def on_device(images, variances, valid, psf_sigma, offsets):
    epochs = images.shape[0]
    tile = images.shape[-1]
    sky = lax.axis_size("sky")
    blocks = lax.axis_size("epoch")
    block = VELS // (blocks * lax.axis_size("vel"))
    exchange = sky == GRID_X
    last_epoch = epochs * blocks * lax.axis_size("vel") - 1
    runs = 1 + 2 * -(-REACH * (epochs - 1) // last_epoch)
    rows_out = -(-(tile + 2 * REACH) // 16) * 16
    devices = blocks * lax.axis_size("vel")
    reaches = [PSFR + -(-REACH * ((at + 1) * epochs - 1) // last_epoch) for at in range(devices)]
    widths = [(wide, LANES // wide // 2 * 2) for wide in reaches]
    slots = max(each for _, each in widths)
    smem = pl.BlockSpec(memory_space=pltpu.SMEM)
    vmem = pl.BlockSpec(memory_space=pltpu.VMEM)
    dma = pltpu.SemaphoreType.DMA
    half = blocks * block
    far = max(1, (blocks - 1) * block)
    scratch = [
        pltpu.VMEM((2 * (epochs + 1), rows_out, LANES), jnp.float32),
        pltpu.VMEM((2 * (epochs + 1), rows_out, LANES), jnp.float32),
        pltpu.SMEM((VELS, LANES), jnp.int32),
        pltpu.VMEM((VELS, LANES), jnp.int32),
        dma(()),
        pltpu.VMEM((rows_out, tile if exchange else tile + LANES), jnp.float32),
        pltpu.VMEM((LANES, 2 * LANES), jnp.float32),
        pltpu.VMEM((slots if exchange else 1, LANES, 2 * LANES), jnp.float32),
        pltpu.VMEM((2, 2, 2 * LANES, 2 * LANES), jnp.bfloat16),
        pltpu.VMEM((half, 2, tile, tile), jnp.bfloat16),
        pltpu.VMEM((half, 2, tile, tile), jnp.bfloat16),
        pltpu.VMEM((far, 2, tile, tile), jnp.bfloat16),
        pltpu.VMEM((far, 2, tile, tile), jnp.bfloat16),
        pltpu.VMEM((2, block, 2, tile, tile), jnp.float32),
        dma((half,)), dma((half,)), dma((far,)), dma((far,)),
    ]
    if exchange:
        groups = -(-epochs // min(each for _, each in widths))
        scratch += [
            pltpu.VMEM((epochs, 2, tile, tile), jnp.bfloat16),
            pltpu.VMEM((2, 2, tile, LANES), jnp.float32),
            pltpu.VMEM((2, groups, 2, tile, LANES), jnp.bfloat16),
            pltpu.VMEM((2, groups, 2, tile, LANES), jnp.bfloat16),
            dma((2, groups)), dma((2, groups)),
        ]
        operands = (offsets, offsets, psf_sigma, valid.reshape(epochs), images, variances)
        in_specs = [smem, vmem, smem, smem, vmem, vmem]
    else:
        usable = valid[:, 0].astype(jnp.float32)[:, None, None]
        inverse = usable / variances[:, 0].astype(jnp.float32)
        scaled = images[:, 0].astype(jnp.float32) * inverse
        own = jnp.stack([scaled.astype(jnp.bfloat16), inverse.astype(jnp.bfloat16)], axis=1)
        operands = (offsets, offsets, psf_sigma) + strips(own, sky, tile)
        in_specs = [smem, vmem, smem, vmem, vmem]
    out = jax.ShapeDtypeStruct((block, tile, tile), jnp.float32)
    psi_sum, phi_sum = pl.pallas_call(
        functools.partial(fused_kernel, (tile, sky, blocks, block, epochs, runs, widths, exchange)),
        out_shape=(out, out),
        in_specs=in_specs,
        out_specs=(vmem, vmem),
        scratch_shapes=scratch,
        compiler_params=pltpu.CompilerParams(
            collective_id=0, has_side_effects=True, vmem_limit_bytes=56 * 2**20
        ),
    )(*operands)
    phi_sum = jnp.maximum(phi_sum, phi_floor)
    likelihood = psi_sum / jnp.sqrt(phi_sum)
    flux = psi_sum / phi_sum
    return (likelihood[:, None], flux[:, None])


def solution(mesh):
    placed = (
        P(("epoch", "vel"), ("field", "sky"), None, None),
        P(("epoch", "vel"), ("field", "sky"), None, None),
        P(("epoch", "vel"), ("field", "sky")),
        P(("field", "epoch", "vel")),
        P(None, None, "epoch"),
    )
    return jax.shard_map(
        on_device,
        mesh=mesh,
        in_specs=placed,
        out_specs=(
            P(("epoch", "vel"), ("field", "sky"), None, None),
            P(("epoch", "vel"), ("field", "sky"), None, None),
        ),
        check_vma=False,
    )
```

profile of v0, /device:TPU:0, one launch (start us, length us, event | category | flops | bytes accessed | tf_op | source)
XLA Modules:
  0.0 30.7 jit_solution(16817976237050711196)
XLA Ops:
  0.6 28.1 %shard_map.68 = (f32[4,128,128]{2,1,0:T(8,128)}, f32[4,128,128]{2,1,0:T(8,128)}) custom-call(s32[2,16,32]{2,1,0:T(8,128)} %refs_1_.1, s32[2,16,32]{2,1,0:T(8,128)} %refs_1_.1, f32[16]{0:T(128)} %refs_2_.1, s32[16]{0:T(128)} %bitcast.9, bf16[16,1,128,128]{3,2,1,0:T(8,128)(2,1)} %refs_4_.1, bf16[16,1,128,128]{3,2,1,0:T(8,128)(2,1)} %refs_5_.1), custom_call_target="tpu_custom_call" | custom-call | tf_op jit(solution)/shard_map/pallas_call | solution.py:427
  28.8 1.9 %divide_bitcast_fusion = (f32[4,1,128,128]{3,2,1,0:T(8,128)}, f32[4,1,128,128]{3,2,1,0:T(8,128)}) fusion(f32[4,128,128]{2,1,0:T(8,128)} %get-tuple-element.4, f32[4,128,128]{2,1,0:T(8,128)} %get-tuple-element.5), kind=kLoop, calls=%fused_computation | loop fusion | flops 196608 | bytes 1048576
where the time goes:
time: 30.8 us; the launch traced here: 30.7 us
  Pallas kernels  28.1 us (91%)
  other arithmetic  1.89 us (6%)
  between operations  0.64 us (2%)
    pallas_call x1, Pallas kernels, on_device(): pl.pallas_call(functools.partial(fused_kernel, (tile, sky, blocks, block,...  28.1 us
    unnamed x1, other arithmetic  1.89 us

commit v1 on v0

v1 whole, which is shorter than its diff:
```python
import functools

import jax
import jax.numpy as jnp
from jax import lax
from jax.experimental import pallas as pl
from jax.experimental.pallas import tpu as pltpu
from jax.sharding import PartitionSpec as P

VELS = 16
REACH = 12
PSFR = 7
GRID_X = 4
MARGIN = REACH + PSFR
LANES = 128
HEAD = 16
PACK = 16
BACK = 32
EDGE = 32

phi_floor = 0.25


def shifted(block, axis, distance):
    devices = range(lax.axis_size(axis))
    route = [((i - distance) % len(devices), i) for i in devices]
    return lax.ppermute(block, axis, route)


def positions(index, tile):
    return jnp.where(
        index < tile,
        index,
        jnp.where(
            index < tile + MARGIN,
            index - tile - MARGIN,
            jnp.where(index < tile + 2 * MARGIN, index - MARGIN, 4 * tile),
        ),
    )


FAR = -1.0e9


def exponents(distance):
    away = distance.astype(jnp.float32)
    return jnp.where(jnp.abs(distance) <= PSFR, -0.5 * away * away, FAR)


def fused_kernel(plan, *refs):
    tile, sky, blocks, block, epochs, runs = plan
    (offsets, motion, sigmas, own, halo, psi_out, phi_out, plane_a, plane_b, ends, ends_made, ends_sem, row_q,
     own_q, side_q, bands, send_v, recv_v, send_x, recv_x, keep, sv, rv, sx, rx) = refs
    maps = 2
    rows_in = row_q.shape[1]
    rows_out = plane_a.shape[1]
    width = 2 * LANES
    mesh_id = pl.DeviceIdType.MESH
    group = lax.axis_index("epoch")
    member = lax.axis_index("vel")
    partner = 1 - member

    barrier = pltpu.get_barrier_semaphore()
    greeted = 1
    pl.semaphore_signal(barrier, inc=1, device_id={"vel": partner}, device_id_type=mesh_id)
    for a in range(1, blocks):
        peer = lax.rem(group + a, blocks)
        pl.semaphore_signal(barrier, inc=1, device_id={"epoch": peer}, device_id_type=mesh_id)
        greeted += 1
    pl.semaphore_wait(barrier, greeted)

    shape = (rows_out, rows_in)
    row_q[...] = exponents(
        positions(lax.broadcasted_iota(jnp.int32, shape, 1), tile)
        - lax.broadcasted_iota(jnp.int32, shape, 0) + REACH
    )
    shape = (LANES, width)
    held = lax.broadcasted_iota(jnp.int32, shape, 0)
    shifted_out = lax.broadcasted_iota(jnp.int32, shape, 1) - REACH
    own_q[...] = exponents(held - shifted_out)
    side_q[0] = exponents(positions(held + tile, tile) - shifted_out)

    first = member * epochs

    at_epoch = lax.broadcasted_iota(jnp.int32, motion.shape[1:], 1)
    moved = jnp.zeros(motion.shape[1:], jnp.int32)
    for way in range(2):
        start = jnp.where(at_epoch == first, motion[way], 0)
        moved += jnp.abs(motion[way] - jnp.sum(start, axis=1, keepdims=True))
    held_here = (at_epoch >= first) & (at_epoch < first + epochs)
    counted = jnp.zeros(ends_made.shape, jnp.int32)
    at_run = lax.broadcasted_iota(jnp.int32, ends_made.shape, 1)
    for run in range(runs - 1):
        count = jnp.sum((held_here & (moved <= run)).astype(jnp.int32), axis=1, keepdims=True)
        counted = jnp.where(at_run == run, count, counted)
    ends_made[...] = counted
    ends_copy = pltpu.make_async_copy(ends_made, ends, ends_sem)
    ends_copy.start()
    plane_a[:maps] = jnp.zeros_like(plane_a[:maps])
    plane_b[:maps] = jnp.zeros_like(plane_b[:maps])

    def correlate(e, turn):
        sigma = jnp.full((8, LANES), sigmas[e], jnp.float32)
        power = 1.0 / (sigma * sigma)
        tap = lax.broadcasted_iota(jnp.int32, (8, LANES), 1) - PSFR
        norm = jnp.sum(jnp.exp(exponents(tap) * power), axis=1, keepdims=True)
        scale = (1.0 / norm)[:1]
        power = power[:1, :1]

        def both(q):
            profile = jnp.exp(q * power) * scale
            return profile.astype(jnp.bfloat16), (profile * profile).astype(jnp.bfloat16)

        row_bands = both(row_q[...])
        for part, q in enumerate((own_q[...], side_q[0])):
            for m, made in enumerate(both(q)):
                bands[turn, m, part * LANES : (part + 1) * LANES] = made
        for m in range(maps):
            side = halo[e, m]
            held = jnp.concatenate([own[e, m], side], axis=1)
            rows = jnp.dot(row_bands[m], held, preferred_element_type=jnp.float32)
            done = jnp.dot(
                rows.astype(jnp.bfloat16), bands[turn, m], preferred_element_type=jnp.float32
            )
            at = maps * e + m
            plane_a[at + maps] = plane_a[at] + done[:, :LANES]
            plane_b[at + maps] = plane_b[at] + done[:, LANES:]

    step = 2 if epochs % 2 == 0 else 1

    def several(i, carry):
        for turn in range(step):
            correlate(step * i + turn, turn)
        return carry

    lax.fori_loop(0, epochs // step, several, 0)

    def vel_copy(at):
        return pltpu.make_async_remote_copy(
            src_ref=send_v.at[at], dst_ref=recv_v.at[at], send_sem=sv.at[at], recv_sem=rv.at[at],
            device_id={"vel": partner}, device_id_type=mesh_id,
        )

    def epoch_copy(at):
        peer = lax.rem(group + 1 + at // block, blocks)
        return pltpu.make_async_remote_copy(
            src_ref=send_x.at[at], dst_ref=recv_x.at[at], send_sem=sx.at[at], recv_sem=rx.at[at],
            device_id={"epoch": peer}, device_id_type=mesh_id,
        )

    def stack(slot, carry):
        a = blocks - 1 - slot // (2 * block)
        turn = lax.rem(slot, 2 * block)
        mine = ((turn > 0) & (lax.rem(turn, 2) == 0)) | (turn == 2 * block - 1)
        b = jnp.where(mine, 0, 1)
        j = jnp.where(turn == 2 * block - 1, block - 1, jnp.where(mine, turn // 2 - 1, (turn + 1) // 2))
        place = a * block + j
        k = (lax.rem(group + a, blocks) * 2 + lax.rem(member + b, 2)) * block + j
        lane = lax.broadcasted_iota(jnp.int32, (tile, LANES), 1)
        summed = [jnp.zeros((tile, LANES), jnp.float32) for _ in range(maps)]
        low = jnp.zeros((), jnp.int32)
        for run in range(runs):
            high = ends[k, run] if run < runs - 1 else epochs
            at = first + jnp.minimum(low, epochs - 1)
            down = offsets[0, k, at] + REACH
            right = offsets[1, k, at] + REACH
            rows = pl.ds(down, tile)
            for m in range(maps):
                left_part = plane_a[maps * high + m, rows, :] - plane_a[maps * low + m, rows, :]
                right_part = plane_b[maps * high + m, rows, :] - plane_b[maps * low + m, rows, :]
                merged = jnp.where(lane >= right, left_part, right_part)
                summed[m] += pltpu.roll(merged, LANES - right, axis=1)
            low = high
        for m in range(maps):
            keep[b, j, m] = summed[m]

        @pl.when(b == 1)
        def _():
            send_v[place] = keep[1, j].astype(jnp.bfloat16)
            vel_copy(place).start()

        @pl.when(b == 0)
        def _():
            vel_copy(place).wait_recv()
            keep[0, j] = keep[0, j] + recv_v[place].astype(jnp.float32)

            @pl.when(a > 0)
            def _():
                send_x[place - block] = keep[0, j].astype(jnp.bfloat16)
                epoch_copy(place - block).start()

        return carry

    ends_copy.wait()
    lax.fori_loop(0, 2 * blocks * block, stack, 0)

    def finish(j, carry):
        total = keep[0, j]
        for a in range(1, blocks):
            at = (a - 1) * block + j
            epoch_copy(at).wait_recv()
            total = total + recv_x[at].astype(jnp.float32)
        psi_out[j] = total[0]
        phi_out[j] = total[1]
        return carry

    lax.fori_loop(0, block, finish, 0)

    def drain_v(at, carry):
        vel_copy(at).wait_send()
        return carry

    lax.fori_loop(0, blocks * block, drain_v, 0)

    def drain_x(at, carry):
        epoch_copy(at).wait_send()
        return carry

    lax.fori_loop(0, (blocks - 1) * block, drain_x, 0)


def strips(own, tile_count, tile):
    position = (lax.axis_index("sky") + GRID_X // 2) % tile_count
    column = position % GRID_X
    left = shifted(own[..., tile - MARGIN :], "sky", 1)
    right = shifted(own[..., :MARGIN], "sky", -1)
    left = jnp.where(column > 0, left, jnp.zeros_like(left))
    right = jnp.where(column < GRID_X - 1, right, jnp.zeros_like(right))
    blank = jnp.zeros(own.shape[:3] + (LANES - 2 * MARGIN,), jnp.bfloat16)
    both = jnp.concatenate([own, left, right, blank], axis=3)
    upper = shifted(both[:, :, tile - MARGIN :], "sky", GRID_X)
    lower = shifted(both[:, :, :MARGIN], "sky", -GRID_X)
    upper = jnp.where(position >= GRID_X, upper, jnp.zeros_like(upper))
    lower = jnp.where(position < tile_count - GRID_X, lower, jnp.zeros_like(lower))
    blank = jnp.zeros(both.shape[:2] + (LANES - 2 * MARGIN, both.shape[3]), jnp.bfloat16)
    both = jnp.concatenate([both, upper, lower, blank], axis=2)
    return both[..., :tile], both[..., tile:]


def near_kernel(plan, *refs):
    tile, sky, blocks, block, epochs, runs, slots = plan
    (offsets, motion, sigmas, valid, images, variances, psi_out, phi_out, plane, edge, ends, ends_made, ends_sem,
     image, variance, load_sem, place, shift, row_q, own_q, near_q, far_q, own, sent, came, sz, rz,
     send_v, recv_v, send_x, recv_x, keep, sv, rv, sx, rx) = refs
    maps = 2
    groups = -(-epochs // slots)
    rows_out = row_q.shape[0]
    mesh_id = pl.DeviceIdType.MESH
    me = lax.axis_index("sky")
    group = lax.axis_index("epoch")
    member = lax.axis_index("vel")
    column = lax.rem(lax.rem(me + GRID_X // 2, sky), GRID_X)
    before = lax.rem(me + sky - 1, sky)
    after = lax.rem(me + 1, sky)
    partner = 1 - member

    barrier = pltpu.get_barrier_semaphore()
    greeted = 3
    pl.semaphore_signal(barrier, inc=1, device_id={"vel": partner}, device_id_type=mesh_id)
    for a in range(1, blocks):
        peer = lax.rem(group + a, blocks)
        pl.semaphore_signal(barrier, inc=1, device_id={"epoch": peer}, device_id_type=mesh_id)
        greeted += 1
    for other in (before, after):
        pl.semaphore_signal(barrier, inc=1, device_id={"sky": other}, device_id_type=mesh_id)

    def members(g):
        return range(g * slots, min((g + 1) * slots, epochs))

    def load(which, g):
        source, held = ((images, image), (variances, variance))[which]
        span = pl.ds(g * slots, len(members(g)))
        return pltpu.make_async_copy(source.at[span, 0], held.at[span], load_sem.at[which, g])

    for g in range(groups):
        for which in range(2):
            load(which, g).start()

    def iota(shape, axis):
        return lax.broadcasted_iota(jnp.int32, shape, axis)

    def one_hot(hit):
        return jnp.where(hit, 1.0, 0.0).astype(jnp.bfloat16)

    lane = iota((tile, LANES), 1)
    row = iota((tile, LANES), 0)

    def make_place(s, carry):
        low = lane - (slot_start(s) + MARGIN + BACK)
        place[s, :, :LANES] = one_hot((row < MARGIN) & (((low - row) & (LANES - 1)) == 0))
        high = lane - slot_start(s)
        place[s, :, LANES:] = one_hot((row >= tile - MARGIN) & (high == row - (tile - MARGIN)))
        return carry

    def slot_start(s):
        return MARGIN * s

    lax.fori_loop(0, slots, make_place, 0)

    def side_copy(to_after, g):
        return pltpu.make_async_remote_copy(
            src_ref=sent.at[to_after, g],
            dst_ref=came.at[to_after, g],
            send_sem=sz.at[to_after, g],
            recv_sem=rz.at[to_after, g],
            device_id={"sky": after if to_after else before},
            device_id_type=mesh_id,
        )

    for g in range(groups):
        for which in range(2):
            load(which, g).wait()
        for e in members(g):
            usable = valid[e].astype(jnp.float32)
            inverse = usable / variance[e].astype(jnp.float32)
            scaled = image[e].astype(jnp.float32) * inverse
            own[e, 0] = scaled.astype(jnp.bfloat16)
            own[e, 1] = inverse.astype(jnp.bfloat16)
        spread = jnp.concatenate([place[s] for s in range(len(members(g)))], axis=0)
        for m in range(maps):
            strip = jnp.concatenate([own[e, m] for e in members(g)], axis=1)
            placed = jnp.dot(strip, spread, preferred_element_type=jnp.float32)
            sent[0, g, m] = placed[:, :LANES].astype(jnp.bfloat16)
            sent[1, g, m] = placed[:, LANES:].astype(jnp.bfloat16)
        if g == 0:
            pl.semaphore_wait(barrier, greeted)

        @pl.when(column > 0)
        def _():
            side_copy(0, g).start()

        @pl.when(column < GRID_X - 1)
        def _():
            side_copy(1, g).start()

    @pl.when(column == 0)
    def _():
        came[1] = jnp.zeros_like(came[1])

    @pl.when(column == GRID_X - 1)
    def _():
        came[0] = jnp.zeros_like(came[0])

    def make_shift(at, carry):
        shift[at] = one_hot(row == lane + (at - REACH))
        return carry

    lax.fori_loop(0, 2 * REACH + 1, make_shift, 0)

    row_q[...] = exponents(iota(row_q.shape, 1) - iota(row_q.shape, 0) + HEAD)

    def edge_index(shape):
        return ((iota(shape, 1) + EDGE // 2) & (EDGE - 1)) - EDGE // 2

    def edge_column(shape):
        index = edge_index(shape)
        beyond = jnp.where(index < 0, index, index + tile)
        return jnp.where((index >= -REACH) & (index < REACH), beyond, 4 * tile)

    def side_pixel(kept):
        left = (kept >= BACK - MARGIN) & (kept < BACK)
        right = (kept >= 2 * BACK) & (kept < 2 * BACK + MARGIN)
        return jnp.where(left, kept - BACK, jnp.where(right, kept - 2 * BACK + tile, -4 * tile))

    at = iota(own_q.shape, 0)
    own_q[...] = exponents(jnp.where(at < PACK, at, at + tile - 2 * PACK) - edge_column(own_q.shape))
    at = iota(near_q.shape, 0)
    kept = jnp.where(at < PACK, at + BACK - PACK, at - PACK + 2 * BACK)
    near_q[...] = exponents(side_pixel(kept) - iota(near_q.shape, 1))
    at = iota(far_q.shape, 0)
    kept = jnp.where(at < BACK, at, at + BACK)
    far_q[...] = exponents(side_pixel(kept) - edge_column(far_q.shape))

    first = member * epochs
    at_epoch = iota(motion.shape[1:], 1)
    moved = jnp.zeros(motion.shape[1:], jnp.int32)
    for way in range(2):
        start = jnp.where(at_epoch == first, motion[way], 0)
        moved += jnp.abs(motion[way] - jnp.sum(start, axis=1, keepdims=True))
    held_here = (at_epoch >= first) & (at_epoch < first + epochs)
    counted = jnp.zeros(ends_made.shape, jnp.int32)
    at_run = iota(ends_made.shape, 1)
    for run in range(runs - 1):
        count = jnp.sum((held_here & (moved <= run)).astype(jnp.int32), axis=1, keepdims=True)
        counted = jnp.where(at_run == run, count, counted)
    ends_made[...] = counted
    ends_copy = pltpu.make_async_copy(ends_made, ends, ends_sem)
    ends_copy.start()
    plane[:maps] = jnp.zeros_like(plane[:maps])
    edge[:maps] = jnp.zeros_like(edge[:maps])

    parts = tile // EDGE
    edge_rows = edge.shape[1]
    edge_group = iota((edge_rows, LANES), 1) + EDGE // 2
    edge_group = (edge_group & (LANES - 1)) // EDGE

    def correlate(e, g, s):
        sigma = jnp.full((8, LANES), sigmas[e], jnp.float32)
        power = 1.0 / (sigma * sigma)
        tap = iota((8, LANES), 1) - PSFR
        norm = jnp.sum(jnp.exp(exponents(tap) * power), axis=1, keepdims=True)
        scale = (1.0 / norm)[:1]
        power = power[:1, :1]

        def both(q):
            profile = jnp.exp(q * power) * scale
            return profile.astype(jnp.bfloat16), (profile * profile).astype(jnp.bfloat16)

        row_bands, own_bands, near_bands, far_bands = (both(q[...]) for q in (row_q, own_q, near_q, far_q))

        def blank(rows):
            return jnp.zeros((rows, LANES), jnp.bfloat16)

        window = slot_start(s)
        in_slot = (lane >= window) & (lane < window + MARGIN)
        turn = (2 * LANES + BACK - MARGIN - window) & (LANES - 1)
        for m in range(maps):
            from_own = jnp.concatenate(
                [
                    row_bands[m][HEAD : HEAD + tile],
                    jnp.concatenate(
                        [own_bands[m][:PACK], blank(tile - 2 * PACK), own_bands[m][PACK:]], axis=0
                    ),
                ],
                axis=1,
            )
            near = [
                blank(BACK - PACK), near_bands[m][:PACK], blank(BACK),
                near_bands[m][PACK:], blank(2 * BACK - PACK),
            ]
            far = [far_bands[m][:BACK], blank(BACK), far_bands[m][BACK:], blank(BACK)]
            from_side = jnp.concatenate([jnp.concatenate(near, axis=0), jnp.concatenate(far, axis=0)], axis=1)
            side = jnp.where(in_slot, came[1, g, m].astype(jnp.float32), came[0, g, m].astype(jnp.float32))
            side = pltpu.roll(side, turn, axis=1).astype(jnp.bfloat16)
            held = jnp.concatenate([own[e, m], side], axis=1)
            columns = jnp.dot(
                held, jnp.concatenate([from_own, from_side], axis=0), preferred_element_type=jnp.float32
            )
            done = jnp.dot(row_bands[m], columns.astype(jnp.bfloat16), preferred_element_type=jnp.float32)
            slot = maps * e + m
            plane[slot + maps] = plane[slot] + done[:, :LANES]
            beyond = done[:, LANES:]
            packed = beyond[:edge_rows]
            for part in range(1, parts):
                packed = jnp.where(edge_group == part, beyond[EDGE * part : EDGE * part + edge_rows], packed)
            edge[slot + maps] = edge[slot] + packed

    step = 2 if epochs % 2 == 0 and slots % 2 == 0 else 1

    def several(i, carry):
        g = (step * i) // slots

        @pl.when(lax.rem(step * i, slots) == 0)
        def _():
            @pl.when(column < GRID_X - 1)
            def _():
                side_copy(0, g).wait_recv()

            @pl.when(column > 0)
            def _():
                side_copy(1, g).wait_recv()

        for turn in range(step):
            correlate(step * i + turn, g, lax.rem(step * i, slots) + turn)
        return carry

    lax.fori_loop(0, epochs // step, several, 0)

    def vel_copy(at):
        return pltpu.make_async_remote_copy(
            src_ref=send_v.at[at], dst_ref=recv_v.at[at], send_sem=sv.at[at], recv_sem=rv.at[at],
            device_id={"vel": partner}, device_id_type=mesh_id,
        )

    def epoch_copy(at):
        peer = lax.rem(group + 1 + at // block, blocks)
        return pltpu.make_async_remote_copy(
            src_ref=send_x.at[at], dst_ref=recv_x.at[at], send_sem=sx.at[at], recv_sem=rx.at[at],
            device_id={"epoch": peer}, device_id_type=mesh_id,
        )

    index = edge_index((EDGE, LANES))
    near_edge = (lane[:EDGE] < EDGE // 2) | (lane[:EDGE] >= LANES - EDGE // 2)

    def stack(slot, carry):
        a = blocks - 1 - slot // (2 * block)
        turn = lax.rem(slot, 2 * block)
        mine = ((turn > 0) & (lax.rem(turn, 2) == 0)) | (turn == 2 * block - 1)
        b = jnp.where(mine, 0, 1)
        j = jnp.where(turn == 2 * block - 1, block - 1, jnp.where(mine, turn // 2 - 1, (turn + 1) // 2))
        spot = a * block + j
        k = (lax.rem(group + a, blocks) * 2 + lax.rem(member + b, 2)) * block + j
        low = jnp.zeros((), jnp.int32)
        summed = jnp.zeros((maps * tile, LANES), jnp.float32)
        margins = [jnp.zeros((EDGE, LANES), jnp.float32) for _ in range(maps)]
        lefts, rights = [], []
        for run in range(runs):
            high = ends[k, run] if run < runs - 1 else epochs
            at = first + jnp.minimum(low, epochs - 1)
            down = offsets[0, k, at]
            right = offsets[1, k, at]
            rows = pl.ds(down + HEAD, tile)
            few = pl.ds(down + HEAD, EDGE)
            taken = (index >= jnp.minimum(right, 0)) & (index < jnp.maximum(right, 0))
            pieces = []
            for m in range(maps):
                piece = plane[maps * high + m, rows, :]
                rim = edge[maps * high + m, few, :]
                if run > 0:
                    piece = piece - plane[maps * low + m, rows, :]
                    rim = rim - edge[maps * low + m, few, :]
                pieces.append(piece.astype(jnp.bfloat16))
                rim = jnp.where(taken, rim, 0.0)
                margins[m] += pltpu.roll(rim, (LANES - right) & (LANES - 1), axis=1)
            lefts.append(jnp.concatenate(pieces, axis=0))
            rights.append(shift[right + REACH])
            low = high
            if len(lefts) == 2 or run == runs - 1:
                summed += jnp.dot(
                    jnp.concatenate(lefts, axis=1), jnp.concatenate(rights, axis=0),
                    preferred_element_type=jnp.float32,
                )
                lefts, rights = [], []
        for m in range(maps):
            for part in range(parts):
                rim = margins[m] if part == 0 else pltpu.roll(margins[m], LANES - EDGE * part, axis=1)
                begin = EDGE * part
                keep[b, j, m, begin : begin + EDGE] = (
                    summed[m * tile + begin : m * tile + begin + EDGE] + jnp.where(near_edge, rim, 0.0)
                )

        @pl.when(b == 1)
        def _():
            send_v[spot] = keep[1, j].astype(jnp.bfloat16)
            vel_copy(spot).start()

        @pl.when(b == 0)
        def _():
            vel_copy(spot).wait_recv()
            keep[0, j] = keep[0, j] + recv_v[spot].astype(jnp.float32)

            @pl.when(a > 0)
            def _():
                send_x[spot - block] = keep[0, j].astype(jnp.bfloat16)
                epoch_copy(spot - block).start()

        return carry

    ends_copy.wait()
    lax.fori_loop(0, 2 * blocks * block, stack, 0)

    def finish(j, carry):
        total = keep[0, j]
        for a in range(1, blocks):
            at = (a - 1) * block + j
            epoch_copy(at).wait_recv()
            total = total + recv_x[at].astype(jnp.float32)
        psi_out[j] = total[0]
        phi_out[j] = total[1]
        return carry

    lax.fori_loop(0, block, finish, 0)

    def drain_v(at, carry):
        vel_copy(at).wait_send()
        return carry

    lax.fori_loop(0, blocks * block, drain_v, 0)

    def drain_x(at, carry):
        epoch_copy(at).wait_send()
        return carry

    lax.fori_loop(0, (blocks - 1) * block, drain_x, 0)

    for g in range(groups):
        @pl.when(column > 0)
        def _():
            side_copy(0, g).wait_send()

        @pl.when(column < GRID_X - 1)
        def _():
            side_copy(1, g).wait_send()


def near_stacks(images, variances, valid, psf_sigma, offsets, plan):
    tile, sky, blocks, block, epochs, runs, slots = plan
    groups = -(-epochs // slots)
    rows_out = tile + 2 * HEAD
    smem = pl.BlockSpec(memory_space=pltpu.SMEM)
    vmem = pl.BlockSpec(memory_space=pltpu.VMEM)
    anywhere = pl.BlockSpec(memory_space=pl.ANY)
    dma = pltpu.SemaphoreType.DMA
    half = blocks * block
    far = max(1, (blocks - 1) * block)
    narrow, wide = jnp.bfloat16, jnp.float32
    scratch = [
        pltpu.VMEM((2 * (epochs + 1), rows_out, LANES), wide),
        pltpu.VMEM((2 * (epochs + 1), EDGE + 2 * HEAD, LANES), wide),
        pltpu.SMEM((VELS, LANES), jnp.int32),
        pltpu.VMEM((VELS, LANES), jnp.int32),
        dma(()),
        pltpu.VMEM((epochs, tile, tile), narrow),
        pltpu.VMEM((epochs, tile, tile), narrow),
        dma((2, groups)),
        pltpu.VMEM((slots, tile, 2 * LANES), narrow),
        pltpu.VMEM((2 * REACH + 1, tile, LANES), narrow),
        pltpu.VMEM((rows_out, tile), wide),
        pltpu.VMEM((2 * PACK, LANES), wide),
        pltpu.VMEM((2 * PACK, LANES), wide),
        pltpu.VMEM((2 * BACK, LANES), wide),
        pltpu.VMEM((epochs, 2, tile, tile), narrow),
        pltpu.VMEM((2, groups, 2, tile, LANES), narrow),
        pltpu.VMEM((2, groups, 2, tile, LANES), narrow),
        dma((2, groups)), dma((2, groups)),
        pltpu.VMEM((half, 2, tile, tile), narrow),
        pltpu.VMEM((half, 2, tile, tile), narrow),
        pltpu.VMEM((far, 2, tile, tile), narrow),
        pltpu.VMEM((far, 2, tile, tile), narrow),
        pltpu.VMEM((2, block, 2, tile, tile), wide),
        dma((half,)), dma((half,)), dma((far,)), dma((far,)),
    ]
    out = jax.ShapeDtypeStruct((block, tile, tile), jnp.float32)
    return pl.pallas_call(
        functools.partial(near_kernel, plan),
        out_shape=(out, out),
        in_specs=[smem, vmem, smem, smem, anywhere, anywhere],
        out_specs=(vmem, vmem),
        scratch_shapes=scratch,
        compiler_params=pltpu.CompilerParams(
            collective_id=0, has_side_effects=True, vmem_limit_bytes=56 * 2**20
        ),
    )(offsets, offsets, psf_sigma, valid.reshape(epochs), images, variances)


def far_stacks(images, variances, valid, psf_sigma, offsets, plan):
    tile, sky, blocks, block, epochs, runs = plan
    rows_out = -(-(tile + 2 * REACH) // 16) * 16
    smem = pl.BlockSpec(memory_space=pltpu.SMEM)
    vmem = pl.BlockSpec(memory_space=pltpu.VMEM)
    dma = pltpu.SemaphoreType.DMA
    half = blocks * block
    far = max(1, (blocks - 1) * block)
    scratch = [
        pltpu.VMEM((2 * (epochs + 1), rows_out, LANES), jnp.float32),
        pltpu.VMEM((2 * (epochs + 1), rows_out, LANES), jnp.float32),
        pltpu.SMEM((VELS, LANES), jnp.int32),
        pltpu.VMEM((VELS, LANES), jnp.int32),
        dma(()),
        pltpu.VMEM((rows_out, tile + LANES), jnp.float32),
        pltpu.VMEM((LANES, 2 * LANES), jnp.float32),
        pltpu.VMEM((1, LANES, 2 * LANES), jnp.float32),
        pltpu.VMEM((2, 2, 2 * LANES, 2 * LANES), jnp.bfloat16),
        pltpu.VMEM((half, 2, tile, tile), jnp.bfloat16),
        pltpu.VMEM((half, 2, tile, tile), jnp.bfloat16),
        pltpu.VMEM((far, 2, tile, tile), jnp.bfloat16),
        pltpu.VMEM((far, 2, tile, tile), jnp.bfloat16),
        pltpu.VMEM((2, block, 2, tile, tile), jnp.float32),
        dma((half,)), dma((half,)), dma((far,)), dma((far,)),
    ]
    usable = valid[:, 0].astype(jnp.float32)[:, None, None]
    inverse = usable / variances[:, 0].astype(jnp.float32)
    scaled = images[:, 0].astype(jnp.float32) * inverse
    own = jnp.stack([scaled.astype(jnp.bfloat16), inverse.astype(jnp.bfloat16)], axis=1)
    out = jax.ShapeDtypeStruct((block, tile, tile), jnp.float32)
    return pl.pallas_call(
        functools.partial(fused_kernel, plan),
        out_shape=(out, out),
        in_specs=[smem, vmem, smem, vmem, vmem],
        out_specs=(vmem, vmem),
        scratch_shapes=scratch,
        compiler_params=pltpu.CompilerParams(
            collective_id=0, has_side_effects=True, vmem_limit_bytes=56 * 2**20
        ),
    )(offsets, offsets, psf_sigma, *strips(own, sky, tile))


def on_device(images, variances, valid, psf_sigma, offsets):
    epochs = images.shape[0]
    tile = images.shape[-1]
    sky = lax.axis_size("sky")
    blocks = lax.axis_size("epoch")
    block = VELS // (blocks * lax.axis_size("vel"))
    last_epoch = epochs * blocks * lax.axis_size("vel") - 1
    runs = 1 + 2 * -(-REACH * (epochs - 1) // last_epoch)
    plan = (tile, sky, blocks, block, epochs, runs)
    if sky == GRID_X:
        plan += (LANES // MARGIN // 2 * 2,)
        psi_sum, phi_sum = near_stacks(images, variances, valid, psf_sigma, offsets, plan)
    else:
        psi_sum, phi_sum = far_stacks(images, variances, valid, psf_sigma, offsets, plan)
    phi_sum = jnp.maximum(phi_sum, phi_floor)
    likelihood = psi_sum / jnp.sqrt(phi_sum)
    flux = psi_sum / phi_sum
    return (likelihood[:, None], flux[:, None])


def solution(mesh):
    placed = (
        P(("epoch", "vel"), ("field", "sky"), None, None),
        P(("epoch", "vel"), ("field", "sky"), None, None),
        P(("epoch", "vel"), ("field", "sky")),
        P(("field", "epoch", "vel")),
        P(None, None, "epoch"),
    )
    return jax.shard_map(
        on_device,
        mesh=mesh,
        in_specs=placed,
        out_specs=(
            P(("epoch", "vel"), ("field", "sky"), None, None),
            P(("epoch", "vel"), ("field", "sky"), None, None),
        ),
        check_vma=False,
    )
```

time: 30.8 us -> 31.9 us (1.036)
  Pallas kernels: 28.1 us -> 29.1 us
    pallas_call x1, Pallas kernels: 28.1 us -> 29.1 us  [near_stacks(): pl.pallas_call(functools.partial(near_kernel, plan), out_shape=(out, out)...]
where the time goes in v1:
time: 31.9 us; the launch traced here: 31.6 us
  Pallas kernels  29.1 us (91%)
  other arithmetic  1.89 us (6%)
  between operations  0.64 us (2%)
    pallas_call x1, Pallas kernels, near_stacks(): pl.pallas_call(functools.partial(near_kernel, plan), out_shape=(out, out)...  29.1 us
    unnamed x1, other arithmetic  1.89 us

profile of v1, /device:TPU:0, one launch (start us, length us, event | category | flops | bytes accessed | tf_op | source)
XLA Modules:
  0.0 31.6 jit_solution(10952377935000420256)
XLA Ops:
  0.6 29.1 %shard_map.68 = (f32[4,128,128]{2,1,0:T(8,128)}, f32[4,128,128]{2,1,0:T(8,128)}) custom-call(s32[2,16,32]{2,1,0:T(8,128)} %refs_1_.1, s32[2,16,32]{2,1,0:T(8,128)} %refs_1_.1, f32[16]{0:T(128)} %refs_2_.1, s32[16]{0:T(128)} %bitcast.9, bf16[16,1,128,128]{3,2,1,0:T(8,128)(2,1)} %refs_4_.1, bf16[16,1,128,128]{3,2,1,0:T(8,128)(2,1)} %refs_5_.1), custom_call_target="tpu_custom_call" | custom-call | tf_op jit(solution)/shard_map/pallas_call | solution.py:624
  29.7 1.9 %divide_bitcast_fusion = (f32[4,1,128,128]{3,2,1,0:T(8,128)}, f32[4,1,128,128]{3,2,1,0:T(8,128)}) fusion(f32[4,128,128]{2,1,0:T(8,128)} %get-tuple-element.4, f32[4,128,128]{2,1,0:T(8,128)} %get-tuple-element.5), kind=kLoop, calls=%fused_computation | loop fusion | flops 196608 | bytes 1048576

commit v2 on v1

--- a/solution.py
+++ b/solution.py
@@ -15,8 +15,9 @@
 LANES = 128
 HEAD = 16
 PACK = 16
-BACK = 32
-EDGE = 32
+EDGE = 16
+WINDOW = 32
+CHUNK = 4
 
 phi_floor = 0.25
 
@@ -238,13 +239,12 @@
 
 
 def near_kernel(plan, *refs):
-    tile, sky, blocks, block, epochs, runs, slots = plan
+    tile, sky, blocks, block, epochs, runs, chunk = plan
     (offsets, motion, sigmas, valid, images, variances, psi_out, phi_out, plane, edge, ends, ends_made, ends_sem,
-     image, variance, load_sem, place, shift, row_q, own_q, near_q, far_q, own, sent, came, sz, rz,
-     send_v, recv_v, send_x, recv_x, keep, sv, rv, sx, rx) = refs
+     image, variance, load_sem, shift, edge_shift, unplace, row_q, edge_q,
+     send_v, recv_v, send_x, recv_x, keep, strip, send_z, recv_z, passed,
+     sv, rv, sx, rx, sz, rz, sp, rp) = refs
     maps = 2
-    groups = -(-epochs // slots)
-    rows_out = row_q.shape[0]
     mesh_id = pl.DeviceIdType.MESH
     me = lax.axis_index("sky")
     group = lax.axis_index("epoch")
@@ -253,28 +253,32 @@
     before = lax.rem(me + sky - 1, sky)
     after = lax.rem(me + 1, sky)
     partner = 1 - member
+    peer = 1 - group
+    has_before = column > 0
+    has_after = column < GRID_X - 1
 
     barrier = pltpu.get_barrier_semaphore()
-    greeted = 3
     pl.semaphore_signal(barrier, inc=1, device_id={"vel": partner}, device_id_type=mesh_id)
-    for a in range(1, blocks):
-        peer = lax.rem(group + a, blocks)
-        pl.semaphore_signal(barrier, inc=1, device_id={"epoch": peer}, device_id_type=mesh_id)
-        greeted += 1
-    for other in (before, after):
-        pl.semaphore_signal(barrier, inc=1, device_id={"sky": other}, device_id_type=mesh_id)
-
-    def members(g):
-        return range(g * slots, min((g + 1) * slots, epochs))
-
-    def load(which, g):
+    pl.semaphore_signal(barrier, inc=1, device_id={"epoch": peer}, device_id_type=mesh_id)
+
+    @pl.when(has_before)
+    def _():
+        pl.semaphore_signal(barrier, inc=1, device_id={"sky": before}, device_id_type=mesh_id)
+
+    @pl.when(has_after)
+    def _():
+        pl.semaphore_signal(barrier, inc=1, device_id={"sky": after}, device_id_type=mesh_id)
+
+    greeted = 2 + jnp.where(has_before, 1, 0) + jnp.where(has_after, 1, 0)
+
+    def load(which, c):
         source, held = ((images, image), (variances, variance))[which]
-        span = pl.ds(g * slots, len(members(g)))
-        return pltpu.make_async_copy(source.at[span, 0], held.at[span], load_sem.at[which, g])
-
-    for g in range(groups):
+        span = pl.ds(c * chunk, chunk)
+        return pltpu.make_async_copy(source.at[span, 0], held.at[span], load_sem.at[which, c])
+
+    for c in range(epochs // chunk):
         for which in range(2):
-            load(which, g).start()
+            load(which, c).start()
 
     def iota(shape, axis):
         return lax.broadcasted_iota(jnp.int32, shape, axis)
@@ -285,91 +289,39 @@
     lane = iota((tile, LANES), 1)
     row = iota((tile, LANES), 0)
 
-    def make_place(s, carry):
-        low = lane - (slot_start(s) + MARGIN + BACK)
-        place[s, :, :LANES] = one_hot((row < MARGIN) & (((low - row) & (LANES - 1)) == 0))
-        high = lane - slot_start(s)
-        place[s, :, LANES:] = one_hot((row >= tile - MARGIN) & (high == row - (tile - MARGIN)))
-        return carry
-
-    def slot_start(s):
-        return MARGIN * s
-
-    lax.fori_loop(0, slots, make_place, 0)
-
-    def side_copy(to_after, g):
-        return pltpu.make_async_remote_copy(
-            src_ref=sent.at[to_after, g],
-            dst_ref=came.at[to_after, g],
-            send_sem=sz.at[to_after, g],
-            recv_sem=rz.at[to_after, g],
-            device_id={"sky": after if to_after else before},
-            device_id_type=mesh_id,
-        )
-
-    for g in range(groups):
-        for which in range(2):
-            load(which, g).wait()
-        for e in members(g):
-            usable = valid[e].astype(jnp.float32)
-            inverse = usable / variance[e].astype(jnp.float32)
-            scaled = image[e].astype(jnp.float32) * inverse
-            own[e, 0] = scaled.astype(jnp.bfloat16)
-            own[e, 1] = inverse.astype(jnp.bfloat16)
-        spread = jnp.concatenate([place[s] for s in range(len(members(g)))], axis=0)
+    def beyond(lanes):
+        at_left = (lanes >= 0) & (lanes < MARGIN)
+        at_right = (lanes >= WINDOW) & (lanes < WINDOW + MARGIN)
+        return jnp.where(at_left, lanes - MARGIN, jnp.where(at_right, lanes - WINDOW + tile, 8 * tile))
+
+    def edge_column(lanes):
+        index = (lanes & (EDGE - 1)) - EDGE // 2
+        held = (index >= -PSFR) & (index < PSFR)
+        return jnp.where(held, jnp.where(index < 0, index, index + tile), 4 * tile)
+
+    short = iota((EDGE, LANES), 1)
+    from_edge = edge_column(iota((EDGE, LANES), 0))
+
+    def make_shift(at, carry):
+        right = at - REACH
+        shift[at, :, :LANES] = one_hot(row == lane + right)
+        shift[at, :, LANES:] = one_hot(row == beyond(lane) + right)
+        edge_shift[at, :, :LANES] = one_hot(from_edge == short + right)
+        edge_shift[at, :, LANES:] = one_hot(from_edge == beyond(short) + right)
+        return carry
+
+    lax.fori_loop(0, 2 * REACH + 1, make_shift, 0)
+    for odd in range(2):
         for m in range(maps):
-            strip = jnp.concatenate([own[e, m] for e in members(g)], axis=1)
-            placed = jnp.dot(strip, spread, preferred_element_type=jnp.float32)
-            sent[0, g, m] = placed[:, :LANES].astype(jnp.bfloat16)
-            sent[1, g, m] = placed[:, LANES:].astype(jnp.bfloat16)
-        if g == 0:
-            pl.semaphore_wait(barrier, greeted)
-
-        @pl.when(column > 0)
-        def _():
-            side_copy(0, g).start()
-
-        @pl.when(column < GRID_X - 1)
-        def _():
-            side_copy(1, g).start()
-
-    @pl.when(column == 0)
-    def _():
-        came[1] = jnp.zeros_like(came[1])
-
-    @pl.when(column == GRID_X - 1)
-    def _():
-        came[0] = jnp.zeros_like(came[0])
-
-    def make_shift(at, carry):
-        shift[at] = one_hot(row == lane + (at - REACH))
-        return carry
-
-    lax.fori_loop(0, 2 * REACH + 1, make_shift, 0)
+            begin = WINDOW * odd + 2 * WINDOW * m
+            inside = (row >= begin) & (row < begin + MARGIN)
+            unplace[odd, m, :tile] = one_hot(inside & (lane == row - begin))
+            unplace[odd, m, tile:] = one_hot(inside & (lane == row - begin + tile - MARGIN))
 
     row_q[...] = exponents(iota(row_q.shape, 1) - iota(row_q.shape, 0) + HEAD)
-
-    def edge_index(shape):
-        return ((iota(shape, 1) + EDGE // 2) & (EDGE - 1)) - EDGE // 2
-
-    def edge_column(shape):
-        index = edge_index(shape)
-        beyond = jnp.where(index < 0, index, index + tile)
-        return jnp.where((index >= -REACH) & (index < REACH), beyond, 4 * tile)
-
-    def side_pixel(kept):
-        left = (kept >= BACK - MARGIN) & (kept < BACK)
-        right = (kept >= 2 * BACK) & (kept < 2 * BACK + MARGIN)
-        return jnp.where(left, kept - BACK, jnp.where(right, kept - 2 * BACK + tile, -4 * tile))
-
-    at = iota(own_q.shape, 0)
-    own_q[...] = exponents(jnp.where(at < PACK, at, at + tile - 2 * PACK) - edge_column(own_q.shape))
-    at = iota(near_q.shape, 0)
-    kept = jnp.where(at < PACK, at + BACK - PACK, at - PACK + 2 * BACK)
-    near_q[...] = exponents(side_pixel(kept) - iota(near_q.shape, 1))
-    at = iota(far_q.shape, 0)
-    kept = jnp.where(at < BACK, at, at + BACK)
-    far_q[...] = exponents(side_pixel(kept) - edge_column(far_q.shape))
+    at = iota(edge_q.shape, 0)
+    at = jnp.where(at < PACK, at, at + tile - 2 * PACK)
+    edge_q[...] = exponents(at - edge_column(iota(edge_q.shape, 1)))
 
     first = member * epochs
     at_epoch = iota(motion.shape[1:], 1)
@@ -389,12 +341,20 @@
     plane[:maps] = jnp.zeros_like(plane[:maps])
     edge[:maps] = jnp.zeros_like(edge[:maps])
 
-    parts = tile // EDGE
-    edge_rows = edge.shape[1]
-    edge_group = iota((edge_rows, LANES), 1) + EDGE // 2
-    edge_group = (edge_group & (LANES - 1)) // EDGE
-
-    def correlate(e, g, s):
+    @pl.when(column == 0)
+    def _():
+        recv_z[1] = jnp.zeros_like(recv_z[1])
+        passed[1] = jnp.zeros_like(passed[1])
+
+    @pl.when(column == GRID_X - 1)
+    def _():
+        recv_z[0] = jnp.zeros_like(recv_z[0])
+        passed[0] = jnp.zeros_like(passed[0])
+
+    def correlate(e):
+        usable = valid[e].astype(jnp.float32)
+        inverse = usable / variance[e].astype(jnp.float32)
+        scaled = image[e].astype(jnp.float32) * inverse
         sigma = jnp.full((8, LANES), sigmas[e], jnp.float32)
         power = 1.0 / (sigma * sigma)
         tap = iota((8, LANES), 1) - PSFR
@@ -406,62 +366,32 @@
             profile = jnp.exp(q * power) * scale
             return profile.astype(jnp.bfloat16), (profile * profile).astype(jnp.bfloat16)
 
-        row_bands, own_bands, near_bands, far_bands = (both(q[...]) for q in (row_q, own_q, near_q, far_q))
-
-        def blank(rows):
-            return jnp.zeros((rows, LANES), jnp.bfloat16)
-
-        window = slot_start(s)
-        in_slot = (lane >= window) & (lane < window + MARGIN)
-        turn = (2 * LANES + BACK - MARGIN - window) & (LANES - 1)
-        for m in range(maps):
-            from_own = jnp.concatenate(
+        row_bands, edge_bands = both(row_q[...]), both(edge_q[...])
+        for m, field in enumerate((scaled, inverse)):
+            blank = jnp.zeros((tile - 2 * PACK, LANES), jnp.bfloat16)
+            bands = jnp.concatenate(
                 [
                     row_bands[m][HEAD : HEAD + tile],
-                    jnp.concatenate(
-                        [own_bands[m][:PACK], blank(tile - 2 * PACK), own_bands[m][PACK:]], axis=0
-                    ),
+                    jnp.concatenate([edge_bands[m][:PACK], blank, edge_bands[m][PACK:]], axis=0),
                 ],
                 axis=1,
             )
-            near = [
-                blank(BACK - PACK), near_bands[m][:PACK], blank(BACK),
-                near_bands[m][PACK:], blank(2 * BACK - PACK),
-            ]
-            far = [far_bands[m][:BACK], blank(BACK), far_bands[m][BACK:], blank(BACK)]
-            from_side = jnp.concatenate([jnp.concatenate(near, axis=0), jnp.concatenate(far, axis=0)], axis=1)
-            side = jnp.where(in_slot, came[1, g, m].astype(jnp.float32), came[0, g, m].astype(jnp.float32))
-            side = pltpu.roll(side, turn, axis=1).astype(jnp.bfloat16)
-            held = jnp.concatenate([own[e, m], side], axis=1)
-            columns = jnp.dot(
-                held, jnp.concatenate([from_own, from_side], axis=0), preferred_element_type=jnp.float32
-            )
+            columns = jnp.dot(field.astype(jnp.bfloat16), bands, preferred_element_type=jnp.float32)
             done = jnp.dot(row_bands[m], columns.astype(jnp.bfloat16), preferred_element_type=jnp.float32)
             slot = maps * e + m
             plane[slot + maps] = plane[slot] + done[:, :LANES]
-            beyond = done[:, LANES:]
-            packed = beyond[:edge_rows]
-            for part in range(1, parts):
-                packed = jnp.where(edge_group == part, beyond[EDGE * part : EDGE * part + edge_rows], packed)
-            edge[slot + maps] = edge[slot] + packed
-
-    step = 2 if epochs % 2 == 0 and slots % 2 == 0 else 1
+            edge[slot + maps] = edge[slot] + done[:, LANES:]
+
+    step = 2
 
     def several(i, carry):
-        g = (step * i) // slots
-
-        @pl.when(lax.rem(step * i, slots) == 0)
-        def _():
-            @pl.when(column < GRID_X - 1)
-            def _():
-                side_copy(0, g).wait_recv()
-
-            @pl.when(column > 0)
-            def _():
-                side_copy(1, g).wait_recv()
+        @pl.when(lax.rem(step * i, chunk) == 0)
+        def _():
+            for which in range(2):
+                load(which, step * i // chunk).wait()
 
         for turn in range(step):
-            correlate(step * i + turn, g, lax.rem(step * i, slots) + turn)
+            correlate(step * i + turn)
         return carry
 
     lax.fori_loop(0, epochs // step, several, 0)
@@ -473,14 +403,29 @@
         )
 
     def epoch_copy(at):
-        peer = lax.rem(group + 1 + at // block, blocks)
         return pltpu.make_async_remote_copy(
             src_ref=send_x.at[at], dst_ref=recv_x.at[at], send_sem=sx.at[at], recv_sem=rx.at[at],
             device_id={"epoch": peer}, device_id_type=mesh_id,
         )
 
-    index = edge_index((EDGE, LANES))
-    near_edge = (lane[:EDGE] < EDGE // 2) | (lane[:EDGE] >= LANES - EDGE // 2)
+    def side_copy(to_after, at):
+        return pltpu.make_async_remote_copy(
+            src_ref=send_z.at[to_after, at], dst_ref=recv_z.at[to_after, at],
+            send_sem=sz.at[to_after, at], recv_sem=rz.at[to_after, at],
+            device_id={"sky": after if to_after else before}, device_id_type=mesh_id,
+        )
+
+    pairs = block // 2
+
+    def pass_copy(to_after, at):
+        return pltpu.make_async_remote_copy(
+            src_ref=recv_z.at[to_after, pairs + at], dst_ref=passed.at[to_after, at],
+            send_sem=sp.at[to_after, at], recv_sem=rp.at[to_after, at],
+            device_id={"epoch": peer}, device_id_type=mesh_id,
+        )
+
+    part = iota((tile, LANES), 1) // EDGE
+    first_window = (lane & WINDOW) == 0
 
     def stack(slot, carry):
         a = blocks - 1 - slot // (2 * block)
@@ -491,75 +436,112 @@
         spot = a * block + j
         k = (lax.rem(group + a, blocks) * 2 + lax.rem(member + b, 2)) * block + j
         low = jnp.zeros((), jnp.int32)
-        summed = jnp.zeros((maps * tile, LANES), jnp.float32)
-        margins = [jnp.zeros((EDGE, LANES), jnp.float32) for _ in range(maps)]
-        lefts, rights = [], []
+        summed = jnp.zeros((maps * tile, 2 * LANES), jnp.float32)
+        rims = [jnp.zeros((tile, LANES), jnp.float32) for _ in range(maps)]
+        lefts, rights, rim_rights = [], [], []
         for run in range(runs):
             high = ends[k, run] if run < runs - 1 else epochs
             at = first + jnp.minimum(low, epochs - 1)
             down = offsets[0, k, at]
             right = offsets[1, k, at]
             rows = pl.ds(down + HEAD, tile)
-            few = pl.ds(down + HEAD, EDGE)
-            taken = (index >= jnp.minimum(right, 0)) & (index < jnp.maximum(right, 0))
             pieces = []
             for m in range(maps):
                 piece = plane[maps * high + m, rows, :]
-                rim = edge[maps * high + m, few, :]
+                rim = edge[maps * high + m, rows, :]
                 if run > 0:
                     piece = piece - plane[maps * low + m, rows, :]
-                    rim = rim - edge[maps * low + m, few, :]
+                    rim = rim - edge[maps * low + m, rows, :]
                 pieces.append(piece.astype(jnp.bfloat16))
-                rim = jnp.where(taken, rim, 0.0)
-                margins[m] += pltpu.roll(rim, (LANES - right) & (LANES - 1), axis=1)
+                rims[m] = jnp.where(part == run, rim, rims[m])
             lefts.append(jnp.concatenate(pieces, axis=0))
             rights.append(shift[right + REACH])
+            rim_rights.append(edge_shift[right + REACH])
             low = high
-            if len(lefts) == 2 or run == runs - 1:
+            if run == runs - 1:
+                lefts.append(jnp.concatenate([rim.astype(jnp.bfloat16) for rim in rims], axis=0))
+                spare = jnp.zeros((LANES - EDGE * runs, 2 * LANES), jnp.bfloat16)
+                rights.append(jnp.concatenate(rim_rights + [spare], axis=0))
+            while len(lefts) > 1:
                 summed += jnp.dot(
-                    jnp.concatenate(lefts, axis=1), jnp.concatenate(rights, axis=0),
+                    jnp.concatenate(lefts[:2], axis=1), jnp.concatenate(rights[:2], axis=0),
                     preferred_element_type=jnp.float32,
                 )
-                lefts, rights = [], []
-        for m in range(maps):
-            for part in range(parts):
-                rim = margins[m] if part == 0 else pltpu.roll(margins[m], LANES - EDGE * part, axis=1)
-                begin = EDGE * part
-                keep[b, j, m, begin : begin + EDGE] = (
-                    summed[m * tile + begin : m * tile + begin + EDGE] + jnp.where(near_edge, rim, 0.0)
-                )
+                lefts, rights = lefts[2:], rights[2:]
+        outer = summed[:tile, LANES:] + pltpu.roll(summed[tile:, LANES:], 2 * WINDOW, axis=1)
 
         @pl.when(b == 1)
         def _():
-            send_v[spot] = keep[1, j].astype(jnp.bfloat16)
+            for m in range(maps):
+                send_v[spot, m] = summed[m * tile : (m + 1) * tile, :LANES].astype(jnp.bfloat16)
+            send_v[spot, maps] = outer.astype(jnp.bfloat16)
             vel_copy(spot).start()
 
         @pl.when(b == 0)
         def _():
             vel_copy(spot).wait_recv()
-            keep[0, j] = keep[0, j] + recv_v[spot].astype(jnp.float32)
+            for m in range(maps):
+                total = summed[m * tile : (m + 1) * tile, :LANES] + recv_v[spot, m].astype(jnp.float32)
+                keep[spot, m] = total
+            strip[spot] = outer + recv_v[spot, maps].astype(jnp.float32)
 
             @pl.when(a > 0)
             def _():
-                send_x[spot - block] = keep[0, j].astype(jnp.bfloat16)
-                epoch_copy(spot - block).start()
+                send_x[j] = keep[spot].astype(jnp.bfloat16)
+                epoch_copy(j).start()
+
+            @pl.when(lax.rem(j, 2) == 1)
+            def _():
+                even, odd = strip[spot - 1], strip[spot]
+                at = spot // 2
+                send_z[0, at] = jnp.where(first_window, even, pltpu.roll(odd, WINDOW, axis=1)).astype(jnp.bfloat16)
+                send_z[1, at] = jnp.where(first_window, pltpu.roll(even, LANES - WINDOW, axis=1), odd).astype(jnp.bfloat16)
+
+                @pl.when(has_before)
+                def _():
+                    side_copy(0, at).start()
+
+                @pl.when(has_after)
+                def _():
+                    side_copy(1, at).start()
 
         return carry
 
     ends_copy.wait()
+    pl.semaphore_wait(barrier, greeted)
     lax.fori_loop(0, 2 * blocks * block, stack, 0)
 
-    def finish(j, carry):
-        total = keep[0, j]
-        for a in range(1, blocks):
-            at = (a - 1) * block + j
-            epoch_copy(at).wait_recv()
-            total = total + recv_x[at].astype(jnp.float32)
-        psi_out[j] = total[0]
-        phi_out[j] = total[1]
-        return carry
-
-    lax.fori_loop(0, block, finish, 0)
+    for at in range(pairs):
+        @pl.when(has_before)
+        def _():
+            side_copy(1, pairs + at).wait_recv()
+            pass_copy(1, at).start()
+
+        @pl.when(has_after)
+        def _():
+            side_copy(0, pairs + at).wait_recv()
+            pass_copy(0, at).start()
+
+    for at in range(pairs):
+        @pl.when(has_before)
+        def _():
+            side_copy(1, at).wait_recv()
+            pass_copy(1, at).wait_recv()
+
+        @pl.when(has_after)
+        def _():
+            side_copy(0, at).wait_recv()
+            pass_copy(0, at).wait_recv()
+
+        for odd in range(2):
+            j = 2 * at + odd
+            epoch_copy(j).wait_recv()
+            strips_in = jnp.concatenate([recv_z[1, at], recv_z[0, at], passed[1, at], passed[0, at]], axis=1)
+            for m, out in enumerate((psi_out, phi_out)):
+                added = jnp.dot(
+                    strips_in, jnp.concatenate([unplace[odd, m]] * 2, axis=0), preferred_element_type=jnp.float32
+                )
+                out[j] = keep[j, m] + recv_x[j, m].astype(jnp.float32) + added
 
     def drain_v(at, carry):
         vel_copy(at).wait_send()
@@ -571,54 +553,55 @@
         epoch_copy(at).wait_send()
         return carry
 
-    lax.fori_loop(0, (blocks - 1) * block, drain_x, 0)
-
-    for g in range(groups):
-        @pl.when(column > 0)
-        def _():
-            side_copy(0, g).wait_send()
-
-        @pl.when(column < GRID_X - 1)
-        def _():
-            side_copy(1, g).wait_send()
+    lax.fori_loop(0, block, drain_x, 0)
+
+    for to_after, there, back in ((0, has_before, has_after), (1, has_after, has_before)):
+        @pl.when(there)
+        def _():
+            for at in range(blocks * pairs):
+                side_copy(to_after, at).wait_send()
+
+        @pl.when(back)
+        def _():
+            for at in range(pairs):
+                pass_copy(to_after, at).wait_send()
 
 
 def near_stacks(images, variances, valid, psf_sigma, offsets, plan):
-    tile, sky, blocks, block, epochs, runs, slots = plan
-    groups = -(-epochs // slots)
+    tile, sky, blocks, block, epochs, runs, chunk = plan
     rows_out = tile + 2 * HEAD
     smem = pl.BlockSpec(memory_space=pltpu.SMEM)
     vmem = pl.BlockSpec(memory_space=pltpu.VMEM)
     anywhere = pl.BlockSpec(memory_space=pl.ANY)
     dma = pltpu.SemaphoreType.DMA
     half = blocks * block
-    far = max(1, (blocks - 1) * block)
+    pairs = block // 2
     narrow, wide = jnp.bfloat16, jnp.float32
     scratch = [
         pltpu.VMEM((2 * (epochs + 1), rows_out, LANES), wide),
-        pltpu.VMEM((2 * (epochs + 1), EDGE + 2 * HEAD, LANES), wide),
+        pltpu.VMEM((2 * (epochs + 1), rows_out, LANES), wide),
         pltpu.SMEM((VELS, LANES), jnp.int32),
         pltpu.VMEM((VELS, LANES), jnp.int32),
         dma(()),
         pltpu.VMEM((epochs, tile, tile), narrow),
         pltpu.VMEM((epochs, tile, tile), narrow),
-        dma((2, groups)),
-        pltpu.VMEM((slots, tile, 2 * LANES), narrow),
-        pltpu.VMEM((2 * REACH + 1, tile, LANES), narrow),
+        dma((2, epochs // chunk)),
+        pltpu.VMEM((2 * REACH + 1, tile, 2 * LANES), narrow),
+        pltpu.VMEM((2 * REACH + 1, EDGE, 2 * LANES), narrow),
+        pltpu.VMEM((2, 2, 2 * tile, LANES), narrow),
         pltpu.VMEM((rows_out, tile), wide),
         pltpu.VMEM((2 * PACK, LANES), wide),
-        pltpu.VMEM((2 * PACK, LANES), wide),
-        pltpu.VMEM((2 * BACK, LANES), wide),
-        pltpu.VMEM((epochs, 2, tile, tile), narrow),
-        pltpu.VMEM((2, groups, 2, tile, LANES), narrow),
-        pltpu.VMEM((2, groups, 2, tile, LANES), narrow),
-        dma((2, groups)), dma((2, groups)),
-        pltpu.VMEM((half, 2, tile, tile), narrow),
-        pltpu.VMEM((half, 2, tile, tile), narrow),
-        pltpu.VMEM((far, 2, tile, tile), narrow),
-        pltpu.VMEM((far, 2, tile, tile), narrow),
-        pltpu.VMEM((2, block, 2, tile, tile), wide),
-        dma((half,)), dma((half,)), dma((far,)), dma((far,)),
+        pltpu.VMEM((half, 3, tile, tile), narrow),
+        pltpu.VMEM((half, 3, tile, tile), narrow),
+        pltpu.VMEM((block, 2, tile, tile), narrow),
+        pltpu.VMEM((block, 2, tile, tile), narrow),
+        pltpu.VMEM((half, 2, tile, tile), wide),
+        pltpu.VMEM((half, tile, LANES), wide),
+        pltpu.VMEM((2, half // 2, tile, LANES), narrow),
+        pltpu.VMEM((2, half // 2, tile, LANES), narrow),
+        pltpu.VMEM((2, pairs, tile, LANES), narrow),
+        dma((half,)), dma((half,)), dma((block,)), dma((block,)),
+        dma((2, half // 2)), dma((2, half // 2)), dma((2, pairs)), dma((2, pairs)),
     ]
     out = jax.ShapeDtypeStruct((block, tile, tile), jnp.float32)
     return pl.pallas_call(
@@ -684,8 +667,9 @@
     last_epoch = epochs * blocks * lax.axis_size("vel") - 1
     runs = 1 + 2 * -(-REACH * (epochs - 1) // last_epoch)
     plan = (tile, sky, blocks, block, epochs, runs)
-    if sky == GRID_X:
-        plan += (LANES // MARGIN // 2 * 2,)
+    few = EDGE * runs <= LANES and epochs % CHUNK == 0
+    if sky == GRID_X and blocks == 2 and lax.axis_size("vel") == 2 and block % 2 == 0 and few:
+        plan += (CHUNK,)
         psi_sum, phi_sum = near_stacks(images, variances, valid, psf_sigma, offsets, plan)
     else:
         psi_sum, phi_sum = far_stacks(images, variances, valid, psf_sigma, offsets, plan)

time: 31.9 us -> 28.3 us (0.89)
  Pallas kernels: 29.1 us -> 25.6 us
    pallas_call x1, Pallas kernels: 29.1 us -> 25.6 us  [near_stacks(): pl.pallas_call(functools.partial(near_kernel, plan), out_shape=(out, out)...]
where the time goes in v2:
time: 28.3 us; the launch traced here: 28.2 us
  Pallas kernels  25.6 us (90%)
  other arithmetic  1.89 us (7%)
  between operations  0.64 us (2%)
    pallas_call x1, Pallas kernels, near_stacks(): pl.pallas_call(functools.partial(near_kernel, plan), out_shape=(out, out)...  25.6 us
    unnamed x1, other arithmetic  1.89 us

profile of v2, /device:TPU:0, one launch (start us, length us, event | category | flops | bytes accessed | tf_op | source)
XLA Modules:
  0.0 28.2 jit_solution(14162899865627462674)
XLA Ops:
  0.6 25.6 %shard_map.68 = (f32[4,128,128]{2,1,0:T(8,128)}, f32[4,128,128]{2,1,0:T(8,128)}) custom-call(s32[2,16,32]{2,1,0:T(8,128)} %refs_1_.1, s32[2,16,32]{2,1,0:T(8,128)} %refs_1_.1, f32[16]{0:T(128)} %refs_2_.1, s32[16]{0:T(128)} %bitcast.9, bf16[16,1,128,128]{3,2,1,0:T(8,128)(2,1)} %refs_4_.1, bf16[16,1,128,128]{3,2,1,0:T(8,128)(2,1)} %refs_5_.1), custom_call_target="tpu_custom_call" | custom-call | tf_op jit(solution)/shard_map/pallas_call | solution.py:607
  26.3 1.9 %divide_bitcast_fusion = (f32[4,1,128,128]{3,2,1,0:T(8,128)}, f32[4,1,128,128]{3,2,1,0:T(8,128)}) fusion(f32[4,128,128]{2,1,0:T(8,128)} %get-tuple-element.4, f32[4,128,128]{2,1,0:T(8,128)} %get-tuple-element.5), kind=kLoop, calls=%fused_computation | loop fusion | flops 196608 | bytes 1048576

commit v3 on v2

--- a/solution.py
+++ b/solution.py
@@ -18,6 +18,7 @@
 EDGE = 16
 WINDOW = 32
 CHUNK = 4
+KEPT = 55705600
 
 phi_floor = 0.25
 
@@ -382,7 +383,7 @@
             plane[slot + maps] = plane[slot] + done[:, :LANES]
             edge[slot + maps] = edge[slot] + done[:, LANES:]
 
-    step = 2
+    step = 4
 
     def several(i, carry):
         @pl.when(lax.rem(step * i, chunk) == 0)
@@ -427,14 +428,7 @@
     part = iota((tile, LANES), 1) // EDGE
     first_window = (lane & WINDOW) == 0
 
-    def stack(slot, carry):
-        a = blocks - 1 - slot // (2 * block)
-        turn = lax.rem(slot, 2 * block)
-        mine = ((turn > 0) & (lax.rem(turn, 2) == 0)) | (turn == 2 * block - 1)
-        b = jnp.where(mine, 0, 1)
-        j = jnp.where(turn == 2 * block - 1, block - 1, jnp.where(mine, turn // 2 - 1, (turn + 1) // 2))
-        spot = a * block + j
-        k = (lax.rem(group + a, blocks) * 2 + lax.rem(member + b, 2)) * block + j
+    def stacked(k):
         low = jnp.zeros((), jnp.int32)
         summed = jnp.zeros((maps * tile, 2 * LANES), jnp.float32)
         rims = [jnp.zeros((tile, LANES), jnp.float32) for _ in range(maps)]
@@ -469,47 +463,61 @@
                 )
                 lefts, rights = lefts[2:], rights[2:]
         outer = summed[:tile, LANES:] + pltpu.roll(summed[tile:, LANES:], 2 * WINDOW, axis=1)
-
-        @pl.when(b == 1)
-        def _():
-            for m in range(maps):
-                send_v[spot, m] = summed[m * tile : (m + 1) * tile, :LANES].astype(jnp.bfloat16)
-            send_v[spot, maps] = outer.astype(jnp.bfloat16)
-            vel_copy(spot).start()
-
-        @pl.when(b == 0)
-        def _():
-            vel_copy(spot).wait_recv()
-            for m in range(maps):
-                total = summed[m * tile : (m + 1) * tile, :LANES] + recv_v[spot, m].astype(jnp.float32)
-                keep[spot, m] = total
-            strip[spot] = outer + recv_v[spot, maps].astype(jnp.float32)
-
-            @pl.when(a > 0)
+        return summed[:tile, :LANES], summed[tile:, :LANES], outer
+
+    def spot_of(turn):
+        return (blocks - 1 - turn // block) * block + lax.rem(turn, block)
+
+    def finish(turn):
+        spot = spot_of(turn)
+        j = lax.rem(turn, block)
+        vel_copy(spot).wait_recv()
+        for m in range(maps):
+            keep[spot, m] = keep[spot, m] + recv_v[spot, m].astype(jnp.float32)
+        strip[spot] = strip[spot] + recv_v[spot, maps].astype(jnp.float32)
+
+        @pl.when(spot >= block)
+        def _():
+            send_x[j] = keep[spot].astype(jnp.bfloat16)
+            epoch_copy(j).start()
+
+        @pl.when(lax.rem(j, 2) == 1)
+        def _():
+            even, odd = strip[spot - 1], strip[spot]
+            at = spot // 2
+            send_z[0, at] = jnp.where(first_window, even, pltpu.roll(odd, WINDOW, axis=1)).astype(jnp.bfloat16)
+            send_z[1, at] = jnp.where(first_window, pltpu.roll(even, LANES - WINDOW, axis=1), odd).astype(jnp.bfloat16)
+
+            @pl.when(has_before)
             def _():
-                send_x[j] = keep[spot].astype(jnp.bfloat16)
-                epoch_copy(j).start()
-
-            @pl.when(lax.rem(j, 2) == 1)
+                side_copy(0, at).start()
+
+            @pl.when(has_after)
             def _():
-                even, odd = strip[spot - 1], strip[spot]
-                at = spot // 2
-                send_z[0, at] = jnp.where(first_window, even, pltpu.roll(odd, WINDOW, axis=1)).astype(jnp.bfloat16)
-                send_z[1, at] = jnp.where(first_window, pltpu.roll(even, LANES - WINDOW, axis=1), odd).astype(jnp.bfloat16)
-
-                @pl.when(has_before)
-                def _():
-                    side_copy(0, at).start()
-
-                @pl.when(has_after)
-                def _():
-                    side_copy(1, at).start()
+                side_copy(1, at).start()
+
+    def stack(turn, carry):
+        spot = spot_of(turn)
+        owner = lax.rem(group + spot // block, blocks) * 2
+        theirs = stacked((owner + partner) * block + lax.rem(turn, block))
+        mine = stacked((owner + member) * block + lax.rem(turn, block))
+        for m in range(maps + 1):
+            send_v[spot, m] = theirs[m].astype(jnp.bfloat16)
+        vel_copy(spot).start()
+        for m in range(maps):
+            keep[spot, m] = mine[m]
+        strip[spot] = mine[maps]
+
+        @pl.when(turn > 0)
+        def _():
+            finish(turn - 1)
 
         return carry
 
     ends_copy.wait()
     pl.semaphore_wait(barrier, greeted)
-    lax.fori_loop(0, 2 * blocks * block, stack, 0)
+    lax.fori_loop(0, blocks * block, stack, 0)
+    finish(blocks * block - 1)
 
     for at in range(pairs):
         @pl.when(has_before)
@@ -611,7 +619,7 @@
         out_specs=(vmem, vmem),
         scratch_shapes=scratch,
         compiler_params=pltpu.CompilerParams(
-            collective_id=0, has_side_effects=True, vmem_limit_bytes=56 * 2**20
+            collective_id=0, has_side_effects=True, vmem_limit_bytes=KEPT
         ),
     )(offsets, offsets, psf_sigma, valid.reshape(epochs), images, variances)
 

time: 28.3 us -> 26.4 us (0.933)
  Pallas kernels: 25.6 us -> 23.2 us
  local copies, waits for them, and re-layouts: 0 us -> 1.37 us
  other arithmetic: 1.89 us -> 0.87 us
    pallas_call x1, Pallas kernels: 25.6 us -> 23.2 us  [near_stacks(): pl.pallas_call(functools.partial(near_kernel, plan), out_shape=(out, out)...]
    unnamed x0 -> x6, local copies, waits for them, and re-layouts: none -> 1.37 us
    unnamed x1, other arithmetic: 1.89 us -> 0.87 us
where the time goes in v3:
time: 26.4 us; the launch traced here: 26.1 us
  Pallas kernels  23.2 us (88%)
  local copies, waits for them, and re-layouts  1.37 us (5%)
  other arithmetic  0.87 us (3%)
  between operations  0.66 us (2%)
    pallas_call x1, Pallas kernels, near_stacks(): pl.pallas_call(functools.partial(near_kernel, plan), out_shape=(out, out)...  23.2 us
    unnamed x6, local copies, waits for them, and re-layouts  1.37 us
    unnamed x1, other arithmetic  0.87 us

profile of v3, /device:TPU:0, one launch (start us, length us, event | category | flops | bytes accessed | tf_op | source)
XLA Modules:
  0.0 26.1 jit_solution(6620842973444267634)
XLA Ops:
  0.6 0.0 copy-start.1
  0.6 0.0 copy-start.2
  0.7 0.6 %copy-done.1 = f32[16]{0:T(128)S(1)} copy-done((f32[16]{0:T(128)S(1)}, f32[16]{0:T(128)}, u32[]{:S(2)}) %copy-start.1) | copy-done | bytes 88
  1.3 0.0 copy-done.2
  1.3 0.0 copy-start
  1.3 0.7 %copy-done = s32[2,16,32]{2,1,0:T(8,128)S(1)} copy-done((s32[2,16,32]{2,1,0:T(8,128)S(1)}, s32[2,16,32]{2,1,0:T(8,128)}, u32[]{:S(2)}) %copy-start) | copy-done | bytes 4120
  2.0 23.2 %shard_map.68 = (f32[4,128,128]{2,1,0:T(8,128)S(1)}, f32[4,128,128]{2,1,0:T(8,128)S(1)}) custom-call(s32[2,16,32]{2,1,0:T(8,128)S(1)} %copy-done, s32[2,16,32]{2,1,0:T(8,128)S(1)} %copy-done, f32[16]{0:T(128)S(1)} %copy-done.1, s32[16]{0:T(128)S(1)} %bitcast.9, bf16[16,1,128,128]{3,2,1,0:T(8,128)(2,1)} %refs_4_.1, bf16[16,1,128,128]{3,2,1,0:T(8,128)(2,1)} %refs_5_.1), custom_call_target="tpu_custom_call" | custom-call | tf_op jit(solution)/shard_map/pallas_call | solution.py:615
  25.3 0.9 %divide_bitcast_fusion = (f32[4,1,128,128]{3,2,1,0:T(8,128)}, f32[4,1,128,128]{3,2,1,0:T(8,128)}) fusion(f32[4,128,128]{2,1,0:T(8,128)S(1)} %get-tuple-element.4, f32[4,128,128]{2,1,0:T(8,128)S(1)} %get-tuple-element.5), kind=kLoop, calls=%fused_computation | loop fusion | flops 196608 | bytes 1048576
Async XLA Ops:
  0.6 0.7 %copy-start.1 = (f32[16]{0:T(128)S(1)}, f32[16]{0:T(128)}, u32[]{:S(2)}) copy-start(f32[16]{0:T(128)} %refs_2_.1) | copy-start | bytes 196
  0.6 0.7 %copy-start.2 = (s32[16,1]{0,1:T(1,128)S(1)}, s32[16,1]{0,1:T(1,128)}, u32[]{:S(2)}) copy-start(s32[16,1]{0,1:T(1,128)} %param.7) | copy-start | bytes 196
  1.3 0.7 %copy-start = (s32[2,16,32]{2,1,0:T(8,128)S(1)}, s32[2,16,32]{2,1,0:T(8,128)}, u32[]{:S(2)}) copy-start(s32[2,16,32]{2,1,0:T(8,128)} %refs_1_.1) | copy-start | bytes 12292

commit v4 on v3

--- a/solution.py
+++ b/solution.py
@@ -18,6 +18,7 @@
 EDGE = 16
 WINDOW = 32
 CHUNK = 4
+STEP = 2
 KEPT = 55705600
 
 phi_floor = 0.25
@@ -242,7 +243,7 @@
 def near_kernel(plan, *refs):
     tile, sky, blocks, block, epochs, runs, chunk = plan
     (offsets, motion, sigmas, valid, images, variances, psi_out, phi_out, plane, edge, ends, ends_made, ends_sem,
-     image, variance, load_sem, shift, edge_shift, unplace, row_q, edge_q,
+     image, variance, load_sem, shift, edge_shift, unplace, row_q, edge_q, row_bands, edge_bands, columns,
      send_v, recv_v, send_x, recv_x, keep, strip, send_z, recv_z, passed,
      sv, rv, sx, rx, sz, rz, sp, rp) = refs
     maps = 2
@@ -352,50 +353,54 @@
         recv_z[0] = jnp.zeros_like(recv_z[0])
         passed[0] = jnp.zeros_like(passed[0])
 
-    def correlate(e):
-        usable = valid[e].astype(jnp.float32)
-        inverse = usable / variance[e].astype(jnp.float32)
-        scaled = image[e].astype(jnp.float32) * inverse
+    def make_bands(e, carry):
         sigma = jnp.full((8, LANES), sigmas[e], jnp.float32)
         power = 1.0 / (sigma * sigma)
         tap = iota((8, LANES), 1) - PSFR
         norm = jnp.sum(jnp.exp(exponents(tap) * power), axis=1, keepdims=True)
         scale = (1.0 / norm)[:1]
         power = power[:1, :1]
-
-        def both(q):
-            profile = jnp.exp(q * power) * scale
-            return profile.astype(jnp.bfloat16), (profile * profile).astype(jnp.bfloat16)
-
-        row_bands, edge_bands = both(row_q[...]), both(edge_q[...])
+        for q, bands in ((row_q, row_bands), (edge_q, edge_bands)):
+            profile = jnp.exp(q[...] * power) * scale
+            bands[e, 0] = profile.astype(jnp.bfloat16)
+            bands[e, 1] = (profile * profile).astype(jnp.bfloat16)
+        return carry
+
+    lax.fori_loop(0, epochs, make_bands, 0)
+
+    def across(e):
+        usable = valid[e].astype(jnp.float32)
+        inverse = usable / variance[e].astype(jnp.float32)
+        scaled = image[e].astype(jnp.float32) * inverse
+        blank = jnp.zeros((tile - 2 * PACK, LANES), jnp.bfloat16)
         for m, field in enumerate((scaled, inverse)):
-            blank = jnp.zeros((tile - 2 * PACK, LANES), jnp.bfloat16)
-            bands = jnp.concatenate(
-                [
-                    row_bands[m][HEAD : HEAD + tile],
-                    jnp.concatenate([edge_bands[m][:PACK], blank, edge_bands[m][PACK:]], axis=0),
-                ],
-                axis=1,
-            )
-            columns = jnp.dot(field.astype(jnp.bfloat16), bands, preferred_element_type=jnp.float32)
-            done = jnp.dot(row_bands[m], columns.astype(jnp.bfloat16), preferred_element_type=jnp.float32)
+            rims = jnp.concatenate([edge_bands[e, m, :PACK], blank, edge_bands[e, m, PACK:]], axis=0)
+            bands = jnp.concatenate([row_bands[e, m, HEAD : HEAD + tile], rims], axis=1)
+            done = jnp.dot(field.astype(jnp.bfloat16), bands, preferred_element_type=jnp.float32)
+            columns[e, m] = done.astype(jnp.bfloat16)
+
+    def down(e):
+        for m in range(maps):
+            done = jnp.dot(row_bands[e, m], columns[e, m], preferred_element_type=jnp.float32)
             slot = maps * e + m
             plane[slot + maps] = plane[slot] + done[:, :LANES]
             edge[slot + maps] = edge[slot] + done[:, LANES:]
 
-    step = 4
-
-    def several(i, carry):
-        @pl.when(lax.rem(step * i, chunk) == 0)
-        def _():
-            for which in range(2):
-                load(which, step * i // chunk).wait()
-
-        for turn in range(step):
-            correlate(step * i + turn)
-        return carry
-
-    lax.fori_loop(0, epochs // step, several, 0)
+    def all_across(c, carry):
+        for which in range(2):
+            load(which, c).wait()
+        for turn in range(chunk):
+            across(chunk * c + turn)
+        return carry
+
+    lax.fori_loop(0, epochs // chunk, all_across, 0)
+
+    def all_down(c, carry):
+        for turn in range(STEP):
+            down(STEP * c + turn)
+        return carry
+
+    lax.fori_loop(0, epochs // STEP, all_down, 0)
 
     def vel_copy(at):
         return pltpu.make_async_remote_copy(
@@ -468,18 +473,38 @@
     def spot_of(turn):
         return (blocks - 1 - turn // block) * block + lax.rem(turn, block)
 
-    def finish(turn):
+    def owner_of(turn):
+        return lax.rem(group + spot_of(turn) // block, blocks) * 2
+
+    def theirs(turn):
+        return stacked((owner_of(turn) + partner) * block + lax.rem(turn, block))
+
+    def ours(turn):
+        return stacked((owner_of(turn) + member) * block + lax.rem(turn, block))
+
+    def hand_over(turn, parts):
+        spot = spot_of(turn)
+        for m in range(maps + 1):
+            send_v[spot, m] = parts[m].astype(jnp.bfloat16)
+        vel_copy(spot).start()
+
+    def finish(turn, parts):
         spot = spot_of(turn)
         j = lax.rem(turn, block)
         vel_copy(spot).wait_recv()
-        for m in range(maps):
-            keep[spot, m] = keep[spot, m] + recv_v[spot, m].astype(jnp.float32)
-        strip[spot] = strip[spot] + recv_v[spot, maps].astype(jnp.float32)
+        totals = [parts[m] + recv_v[spot, m].astype(jnp.float32) for m in range(maps + 1)]
+        strip[spot] = totals[maps]
 
         @pl.when(spot >= block)
         def _():
-            send_x[j] = keep[spot].astype(jnp.bfloat16)
+            for m in range(maps):
+                send_x[j, m] = totals[m].astype(jnp.bfloat16)
             epoch_copy(j).start()
+
+        @pl.when(spot < block)
+        def _():
+            for m in range(maps):
+                keep[j, m] = totals[m]
 
         @pl.when(lax.rem(j, 2) == 1)
         def _():
@@ -496,28 +521,21 @@
             def _():
                 side_copy(1, at).start()
 
+    last = blocks * block - 1
+
     def stack(turn, carry):
-        spot = spot_of(turn)
-        owner = lax.rem(group + spot // block, blocks) * 2
-        theirs = stacked((owner + partner) * block + lax.rem(turn, block))
-        mine = stacked((owner + member) * block + lax.rem(turn, block))
-        for m in range(maps + 1):
-            send_v[spot, m] = theirs[m].astype(jnp.bfloat16)
-        vel_copy(spot).start()
-        for m in range(maps):
-            keep[spot, m] = mine[m]
-        strip[spot] = mine[maps]
-
-        @pl.when(turn > 0)
-        def _():
-            finish(turn - 1)
-
+        ahead = theirs(turn + 1)
+        kept = ours(turn)
+        hand_over(turn + 1, ahead)
+        finish(turn, kept)
         return carry
 
     ends_copy.wait()
+    ahead = theirs(0)
     pl.semaphore_wait(barrier, greeted)
-    lax.fori_loop(0, blocks * block, stack, 0)
-    finish(blocks * block - 1)
+    hand_over(0, ahead)
+    lax.fori_loop(0, last, stack, 0)
+    finish(last, ours(last))
 
     for at in range(pairs):
         @pl.when(has_before)
@@ -599,11 +617,14 @@
         pltpu.VMEM((2, 2, 2 * tile, LANES), narrow),
         pltpu.VMEM((rows_out, tile), wide),
         pltpu.VMEM((2 * PACK, LANES), wide),
+        pltpu.VMEM((epochs, 2, rows_out, tile), narrow),
+        pltpu.VMEM((epochs, 2, 2 * PACK, LANES), narrow),
+        pltpu.VMEM((epochs, 2, tile, 2 * LANES), narrow),
         pltpu.VMEM((half, 3, tile, tile), narrow),
         pltpu.VMEM((half, 3, tile, tile), narrow),
         pltpu.VMEM((block, 2, tile, tile), narrow),
         pltpu.VMEM((block, 2, tile, tile), narrow),
-        pltpu.VMEM((half, 2, tile, tile), wide),
+        pltpu.VMEM((block, 2, tile, tile), wide),
         pltpu.VMEM((half, tile, LANES), wide),
         pltpu.VMEM((2, half // 2, tile, LANES), narrow),
         pltpu.VMEM((2, half // 2, tile, LANES), narrow),

time: 26.4 us -> 26.3 us (level)
  no operation moved by 1% of the time
where the time goes in v4:
time: 26.3 us; the launch traced here: 26 us
  Pallas kernels  23.2 us (88%)
  local copies, waits for them, and re-layouts  1.37 us (5%)
  other arithmetic  0.87 us (3%)
  between operations  0.66 us (3%)
    pallas_call x1, Pallas kernels, near_stacks(): pl.pallas_call(functools.partial(near_kernel, plan), out_shape=(out, out)...  23.2 us
    unnamed x6, local copies, waits for them, and re-layouts  1.37 us
    unnamed x1, other arithmetic  0.87 us

profile of v4, /device:TPU:0, one launch (start us, length us, event | category | flops | bytes accessed | tf_op | source)
XLA Modules:
  0.0 26.0 jit_solution(4793242713776279300)
XLA Ops:
  0.6 0.0 copy-start.1
  0.6 0.0 copy-start.2
  0.7 0.6 %copy-done.1 = f32[16]{0:T(128)S(1)} copy-done((f32[16]{0:T(128)S(1)}, f32[16]{0:T(128)}, u32[]{:S(2)}) %copy-start.1) | copy-done | bytes 88
  1.3 0.0 copy-done.2
  1.3 0.0 copy-start
  1.3 0.7 %copy-done = s32[2,16,32]{2,1,0:T(8,128)S(1)} copy-done((s32[2,16,32]{2,1,0:T(8,128)S(1)}, s32[2,16,32]{2,1,0:T(8,128)}, u32[]{:S(2)}) %copy-start) | copy-done | bytes 4120
  2.0 23.2 %shard_map.68 = (f32[4,128,128]{2,1,0:T(8,128)S(1)}, f32[4,128,128]{2,1,0:T(8,128)S(1)}) custom-call(s32[2,16,32]{2,1,0:T(8,128)S(1)} %copy-done, s32[2,16,32]{2,1,0:T(8,128)S(1)} %copy-done, f32[16]{0:T(128)S(1)} %copy-done.1, s32[16]{0:T(128)S(1)} %bitcast.9, bf16[16,1,128,128]{3,2,1,0:T(8,128)(2,1)} %refs_4_.1, bf16[16,1,128,128]{3,2,1,0:T(8,128)(2,1)} %refs_5_.1), custom_call_target="tpu_custom_call" | custom-call | tf_op jit(solution)/shard_map/pallas_call | solution.py:636
  25.2 0.9 %divide_bitcast_fusion = (f32[4,1,128,128]{3,2,1,0:T(8,128)}, f32[4,1,128,128]{3,2,1,0:T(8,128)}) fusion(f32[4,128,128]{2,1,0:T(8,128)S(1)} %get-tuple-element.4, f32[4,128,128]{2,1,0:T(8,128)S(1)} %get-tuple-element.5), kind=kLoop, calls=%fused_computation | loop fusion | flops 196608 | bytes 1048576
Async XLA Ops:
  0.6 0.7 %copy-start.1 = (f32[16]{0:T(128)S(1)}, f32[16]{0:T(128)}, u32[]{:S(2)}) copy-start(f32[16]{0:T(128)} %refs_2_.1) | copy-start | bytes 196
  0.6 0.7 %copy-start.2 = (s32[16,1]{0,1:T(1,128)S(1)}, s32[16,1]{0,1:T(1,128)}, u32[]{:S(2)}) copy-start(s32[16,1]{0,1:T(1,128)} %param.7) | copy-start | bytes 196
  1.3 0.7 %copy-start = (s32[2,16,32]{2,1,0:T(8,128)S(1)}, s32[2,16,32]{2,1,0:T(8,128)}, u32[]{:S(2)}) copy-start(s32[2,16,32]{2,1,0:T(8,128)} %refs_1_.1) | copy-start | bytes 12292

commit v5 on v4

--- a/solution.py
+++ b/solution.py
@@ -247,6 +247,7 @@
      send_v, recv_v, send_x, recv_x, keep, strip, send_z, recv_z, passed,
      sv, rv, sx, rx, sz, rz, sp, rp) = refs
     maps = 2
+    rows_out = row_q.shape[0]
     mesh_id = pl.DeviceIdType.MESH
     me = lax.axis_index("sky")
     group = lax.axis_index("epoch")
@@ -334,14 +335,26 @@
     held_here = (at_epoch >= first) & (at_epoch < first + epochs)
     counted = jnp.zeros(ends_made.shape, jnp.int32)
     at_run = iota(ends_made.shape, 1)
-    for run in range(runs - 1):
-        count = jnp.sum((held_here & (moved <= run)).astype(jnp.int32), axis=1, keepdims=True)
-        counted = jnp.where(at_run == run, count, counted)
+    low = jnp.zeros((VELS, 1), jnp.int32)
+    for run in range(runs):
+        high = jnp.full((VELS, 1), epochs, jnp.int32)
+        if run < runs - 1:
+            high = jnp.sum((held_here & (moved <= run)).astype(jnp.int32), axis=1, keepdims=True)
+        begins = at_epoch == first + jnp.minimum(low, epochs - 1)
+        down = jnp.sum(jnp.where(begins, motion[0], 0), axis=1, keepdims=True) + HEAD
+        right = jnp.sum(jnp.where(begins, motion[1], 0), axis=1, keepdims=True) + REACH
+        entries = (
+            maps * rows_out * high + down, maps * rows_out * low + down,
+            rows_out * high + down, rows_out * low + down, right,
+        )
+        for which, entry in enumerate(entries):
+            counted = jnp.where(at_run == EDGE * which + run, entry, counted)
+        low = high
     ends_made[...] = counted
     ends_copy = pltpu.make_async_copy(ends_made, ends, ends_sem)
     ends_copy.start()
-    plane[:maps] = jnp.zeros_like(plane[:maps])
-    edge[:maps] = jnp.zeros_like(edge[:maps])
+    plane[: maps * rows_out] = jnp.zeros((maps * rows_out, LANES), jnp.float32)
+    edge[:rows_out] = jnp.zeros((rows_out, LANES), jnp.float32)
 
     @pl.when(column == 0)
     def _():
@@ -353,7 +366,7 @@
         recv_z[0] = jnp.zeros_like(recv_z[0])
         passed[0] = jnp.zeros_like(passed[0])
 
-    def make_bands(e, carry):
+    def make_bands(e):
         sigma = jnp.full((8, LANES), sigmas[e], jnp.float32)
         power = 1.0 / (sigma * sigma)
         tap = iota((8, LANES), 1) - PSFR
@@ -364,9 +377,13 @@
             profile = jnp.exp(q[...] * power) * scale
             bands[e, 0] = profile.astype(jnp.bfloat16)
             bands[e, 1] = (profile * profile).astype(jnp.bfloat16)
-        return carry
-
-    lax.fori_loop(0, epochs, make_bands, 0)
+
+    def all_bands(c, carry):
+        for turn in range(chunk):
+            make_bands(chunk * c + turn)
+        return carry
+
+    lax.fori_loop(0, epochs // chunk, all_bands, 0)
 
     def across(e):
         usable = valid[e].astype(jnp.float32)
@@ -379,12 +396,19 @@
             done = jnp.dot(field.astype(jnp.bfloat16), bands, preferred_element_type=jnp.float32)
             columns[e, m] = done.astype(jnp.bfloat16)
 
+    own_half = iota((rows_out, LANES), 1) < LANES // 2
+
     def down(e):
+        rims = []
         for m in range(maps):
             done = jnp.dot(row_bands[e, m], columns[e, m], preferred_element_type=jnp.float32)
-            slot = maps * e + m
-            plane[slot + maps] = plane[slot] + done[:, :LANES]
-            edge[slot + maps] = edge[slot] + done[:, LANES:]
+            begin = pl.multiple_of((maps * e + m) * rows_out, 8)
+            ends_at = pl.multiple_of((maps * e + m + maps) * rows_out, 8)
+            plane[pl.ds(ends_at, rows_out)] = plane[pl.ds(begin, rows_out)] + done[:, :LANES]
+            rims.append(done[:, LANES:])
+        begin = pl.multiple_of(e * rows_out, 8)
+        ends_at = pl.multiple_of((e + 1) * rows_out, 8)
+        edge[pl.ds(ends_at, rows_out)] = edge[pl.ds(begin, rows_out)] + jnp.where(own_half, rims[0], rims[1])
 
     def all_across(c, carry):
         for which in range(2):
@@ -430,43 +454,40 @@
             device_id={"epoch": peer}, device_id_type=mesh_id,
         )
 
-    part = iota((tile, LANES), 1) // EDGE
+    each = LANES // (maps * EDGE)
+    part = (lane // EDGE) & (each - 1)
+    low_half = lane < LANES // 2
     first_window = (lane & WINDOW) == 0
 
     def stacked(k):
-        low = jnp.zeros((), jnp.int32)
         summed = jnp.zeros((maps * tile, 2 * LANES), jnp.float32)
-        rims = [jnp.zeros((tile, LANES), jnp.float32) for _ in range(maps)]
+        rims = [jnp.zeros((tile, LANES), jnp.float32) for _ in range(2)]
         lefts, rights, rim_rights = [], [], []
         for run in range(runs):
-            high = ends[k, run] if run < runs - 1 else epochs
-            at = first + jnp.minimum(low, epochs - 1)
-            down = offsets[0, k, at]
-            right = offsets[1, k, at]
-            rows = pl.ds(down + HEAD, tile)
+            high, low, rim_high, rim_low, right = (ends[k, EDGE * which + run] for which in range(5))
+            rim = edge[pl.ds(rim_high, tile), :]
+            if run > 0:
+                rim = rim - edge[pl.ds(rim_low, tile), :]
+            rims[run // each] = jnp.where(part == run % each, rim, rims[run // each])
             pieces = []
             for m in range(maps):
-                piece = plane[maps * high + m, rows, :]
-                rim = edge[maps * high + m, rows, :]
+                piece = plane[pl.ds(high + m * rows_out, tile), :]
                 if run > 0:
-                    piece = piece - plane[maps * low + m, rows, :]
-                    rim = rim - edge[maps * low + m, rows, :]
+                    piece = piece - plane[pl.ds(low + m * rows_out, tile), :]
                 pieces.append(piece.astype(jnp.bfloat16))
-                rims[m] = jnp.where(part == run, rim, rims[m])
             lefts.append(jnp.concatenate(pieces, axis=0))
-            rights.append(shift[right + REACH])
-            rim_rights.append(edge_shift[right + REACH])
-            low = high
-            if run == runs - 1:
-                lefts.append(jnp.concatenate([rim.astype(jnp.bfloat16) for rim in rims], axis=0))
-                spare = jnp.zeros((LANES - EDGE * runs, 2 * LANES), jnp.bfloat16)
-                rights.append(jnp.concatenate(rim_rights + [spare], axis=0))
-            while len(lefts) > 1:
-                summed += jnp.dot(
-                    jnp.concatenate(lefts[:2], axis=1), jnp.concatenate(rights[:2], axis=0),
-                    preferred_element_type=jnp.float32,
-                )
-                lefts, rights = lefts[2:], rights[2:]
+            rights.append(shift[right])
+            rim_rights.append(edge_shift[right])
+        turned = [pltpu.roll(rim, LANES // 2, axis=1) for rim in rims]
+        spread = (jnp.where(low_half, rims[0], turned[1]), jnp.where(low_half, turned[0], rims[1]))
+        lefts.append(jnp.concatenate([rim.astype(jnp.bfloat16) for rim in spread], axis=0))
+        spare = jnp.zeros((LANES - EDGE * runs, 2 * LANES), jnp.bfloat16)
+        rights.append(jnp.concatenate(rim_rights + [spare], axis=0))
+        for run in range(0, len(lefts), 2):
+            summed += jnp.dot(
+                jnp.concatenate(lefts[run : run + 2], axis=1), jnp.concatenate(rights[run : run + 2], axis=0),
+                preferred_element_type=jnp.float32,
+            )
         outer = summed[:tile, LANES:] + pltpu.roll(summed[tile:, LANES:], 2 * WINDOW, axis=1)
         return summed[:tile, :LANES], summed[tile:, :LANES], outer
 
@@ -604,8 +625,8 @@
     pairs = block // 2
     narrow, wide = jnp.bfloat16, jnp.float32
     scratch = [
-        pltpu.VMEM((2 * (epochs + 1), rows_out, LANES), wide),
-        pltpu.VMEM((2 * (epochs + 1), rows_out, LANES), wide),
+        pltpu.VMEM((2 * (epochs + 1) * rows_out, LANES), wide),
+        pltpu.VMEM(((epochs + 1) * rows_out, LANES), wide),
         pltpu.SMEM((VELS, LANES), jnp.int32),
         pltpu.VMEM((VELS, LANES), jnp.int32),
         dma(()),
@@ -696,7 +717,7 @@
     last_epoch = epochs * blocks * lax.axis_size("vel") - 1
     runs = 1 + 2 * -(-REACH * (epochs - 1) // last_epoch)
     plan = (tile, sky, blocks, block, epochs, runs)
-    few = EDGE * runs <= LANES and epochs % CHUNK == 0
+    few = EDGE * runs < LANES and epochs % CHUNK == 0
     if sky == GRID_X and blocks == 2 and lax.axis_size("vel") == 2 and block % 2 == 0 and few:
         plan += (CHUNK,)
         psi_sum, phi_sum = near_stacks(images, variances, valid, psf_sigma, offsets, plan)

time: 26.3 us -> 24.8 us (0.943)
  Pallas kernels: 23.2 us -> 21.7 us
    pallas_call x1, Pallas kernels: 23.2 us -> 21.7 us  [near_stacks(): pl.pallas_call(functools.partial(near_kernel, plan), out_shape=(out, out)...]
where the time goes in v5:
time: 24.8 us; the launch traced here: 24.6 us
  Pallas kernels  21.7 us (88%)
  local copies, waits for them, and re-layouts  1.37 us (6%)
  other arithmetic  0.87 us (4%)
  between operations  0.66 us (3%)
    pallas_call x1, Pallas kernels, near_stacks(): pl.pallas_call(functools.partial(near_kernel, plan), out_shape=(out, out)...  21.7 us
    unnamed x6, local copies, waits for them, and re-layouts  1.37 us
    unnamed x1, other arithmetic  0.87 us

profile of v5, /device:TPU:0, one launch (start us, length us, event | category | flops | bytes accessed | tf_op | source)
XLA Modules:
  0.0 24.6 jit_solution(10728417085359147523)
XLA Ops:
  0.6 0.0 copy-start.1
  0.6 0.0 copy-start.2
  0.7 0.6 %copy-done.1 = f32[16]{0:T(128)S(1)} copy-done((f32[16]{0:T(128)S(1)}, f32[16]{0:T(128)}, u32[]{:S(2)}) %copy-start.1) | copy-done | bytes 88
  1.3 0.0 copy-done.2
  1.3 0.0 copy-start
  1.3 0.7 %copy-done = s32[2,16,32]{2,1,0:T(8,128)S(1)} copy-done((s32[2,16,32]{2,1,0:T(8,128)S(1)}, s32[2,16,32]{2,1,0:T(8,128)}, u32[]{:S(2)}) %copy-start) | copy-done | bytes 4120
  2.0 21.7 %shard_map.68 = (f32[4,128,128]{2,1,0:T(8,128)S(1)}, f32[4,128,128]{2,1,0:T(8,128)S(1)}) custom-call(s32[2,16,32]{2,1,0:T(8,128)S(1)} %copy-done, s32[2,16,32]{2,1,0:T(8,128)S(1)} %copy-done, f32[16]{0:T(128)S(1)} %copy-done.1, s32[16]{0:T(128)S(1)} %bitcast.9, bf16[16,1,128,128]{3,2,1,0:T(8,128)(2,1)} %refs_4_.1, bf16[16,1,128,128]{3,2,1,0:T(8,128)(2,1)} %refs_5_.1), custom_call_target="tpu_custom_call" | custom-call | tf_op jit(solution)/shard_map/pallas_call | solution.py:657
  23.7 0.9 %divide_bitcast_fusion = (f32[4,1,128,128]{3,2,1,0:T(8,128)}, f32[4,1,128,128]{3,2,1,0:T(8,128)}) fusion(f32[4,128,128]{2,1,0:T(8,128)S(1)} %get-tuple-element.4, f32[4,128,128]{2,1,0:T(8,128)S(1)} %get-tuple-element.5), kind=kLoop, calls=%fused_computation | loop fusion | flops 196608 | bytes 1048576
Async XLA Ops:
  0.6 0.7 %copy-start.1 = (f32[16]{0:T(128)S(1)}, f32[16]{0:T(128)}, u32[]{:S(2)}) copy-start(f32[16]{0:T(128)} %refs_2_.1) | copy-start | bytes 196
  0.6 0.7 %copy-start.2 = (s32[16,1]{0,1:T(1,128)S(1)}, s32[16,1]{0,1:T(1,128)}, u32[]{:S(2)}) copy-start(s32[16,1]{0,1:T(1,128)} %param.7) | copy-start | bytes 196
  1.3 0.7 %copy-start = (s32[2,16,32]{2,1,0:T(8,128)S(1)}, s32[2,16,32]{2,1,0:T(8,128)}, u32[]{:S(2)}) copy-start(s32[2,16,32]{2,1,0:T(8,128)} %refs_1_.1) | copy-start | bytes 12292

commit v6 on v5

--- a/solution.py
+++ b/solution.py
@@ -18,7 +18,7 @@
 EDGE = 16
 WINDOW = 32
 CHUNK = 4
-STEP = 2
+STEP = 4
 KEPT = 55705600
 
 phi_floor = 0.25
@@ -242,9 +242,9 @@
 
 def near_kernel(plan, *refs):
     tile, sky, blocks, block, epochs, runs, chunk = plan
-    (offsets, motion, sigmas, valid, images, variances, psi_out, phi_out, plane, edge, ends, ends_made, ends_sem,
+    (motion, sigmas, valid, images, variances, psi_out, phi_out, plane, edge, ends, ends_made, ends_sem,
      image, variance, load_sem, shift, edge_shift, unplace, row_q, edge_q, row_bands, edge_bands, columns,
-     send_v, recv_v, send_x, recv_x, keep, strip, send_z, recv_z, passed,
+     send_v, recv_v, send_x, recv_x, keep, send_z, recv_z, passed,
      sv, rv, sx, rx, sz, rz, sp, rp) = refs
     maps = 2
     rows_out = row_q.shape[0]
@@ -293,9 +293,9 @@
     row = iota((tile, LANES), 0)
 
     def beyond(lanes):
-        at_left = (lanes >= 0) & (lanes < MARGIN)
-        at_right = (lanes >= WINDOW) & (lanes < WINDOW + MARGIN)
-        return jnp.where(at_left, lanes - MARGIN, jnp.where(at_right, lanes - WINDOW + tile, 8 * tile))
+        outward = lanes & (WINDOW - 1)
+        side = jnp.where(lanes < 2 * WINDOW, outward - MARGIN, outward + tile)
+        return jnp.where(outward < MARGIN, side, 8 * tile)
 
     def edge_column(lanes):
         index = (lanes & (EDGE - 1)) - EDGE // 2
@@ -314,12 +314,13 @@
         return carry
 
     lax.fori_loop(0, 2 * REACH + 1, make_shift, 0)
-    for odd in range(2):
-        for m in range(maps):
-            begin = WINDOW * odd + 2 * WINDOW * m
+    for m in range(maps):
+        for bottom in range(2):
+            begin = WINDOW * m + 2 * WINDOW * bottom
             inside = (row >= begin) & (row < begin + MARGIN)
-            unplace[odd, m, :tile] = one_hot(inside & (lane == row - begin))
-            unplace[odd, m, tile:] = one_hot(inside & (lane == row - begin + tile - MARGIN))
+            span = slice(bottom * LANES, (bottom + 1) * LANES)
+            unplace[m, :tile, span] = one_hot(inside & (lane == row - begin))
+            unplace[m, tile:, span] = one_hot(inside & (lane == row - begin + tile - MARGIN))
 
     row_q[...] = exponents(iota(row_q.shape, 1) - iota(row_q.shape, 0) + HEAD)
     at = iota(edge_q.shape, 0)
@@ -445,11 +446,9 @@
             device_id={"sky": after if to_after else before}, device_id_type=mesh_id,
         )
 
-    pairs = block // 2
-
     def pass_copy(to_after, at):
         return pltpu.make_async_remote_copy(
-            src_ref=recv_z.at[to_after, pairs + at], dst_ref=passed.at[to_after, at],
+            src_ref=recv_z.at[to_after, block + at], dst_ref=passed.at[to_after, at],
             send_sem=sp.at[to_after, at], recv_sem=rp.at[to_after, at],
             device_id={"epoch": peer}, device_id_type=mesh_id,
         )
@@ -488,7 +487,7 @@
                 jnp.concatenate(lefts[run : run + 2], axis=1), jnp.concatenate(rights[run : run + 2], axis=0),
                 preferred_element_type=jnp.float32,
             )
-        outer = summed[:tile, LANES:] + pltpu.roll(summed[tile:, LANES:], 2 * WINDOW, axis=1)
+        outer = jnp.where(first_window, summed[:tile, LANES:], summed[tile:, LANES:])
         return summed[:tile, :LANES], summed[tile:, :LANES], outer
 
     def spot_of(turn):
@@ -514,7 +513,18 @@
         j = lax.rem(turn, block)
         vel_copy(spot).wait_recv()
         totals = [parts[m] + recv_v[spot, m].astype(jnp.float32) for m in range(maps + 1)]
-        strip[spot] = totals[maps]
+        upper, lower = totals[maps][: tile // 2], totals[maps][tile // 2 :]
+        to_left = low_half[: tile // 2]
+        send_z[0, spot] = jnp.where(to_left, upper, pltpu.roll(lower, LANES // 2, axis=1)).astype(jnp.bfloat16)
+        send_z[1, spot] = jnp.where(to_left, pltpu.roll(upper, LANES // 2, axis=1), lower).astype(jnp.bfloat16)
+
+        @pl.when(has_before)
+        def _():
+            side_copy(0, spot).start()
+
+        @pl.when(has_after)
+        def _():
+            side_copy(1, spot).start()
 
         @pl.when(spot >= block)
         def _():
@@ -526,21 +536,6 @@
         def _():
             for m in range(maps):
                 keep[j, m] = totals[m]
-
-        @pl.when(lax.rem(j, 2) == 1)
-        def _():
-            even, odd = strip[spot - 1], strip[spot]
-            at = spot // 2
-            send_z[0, at] = jnp.where(first_window, even, pltpu.roll(odd, WINDOW, axis=1)).astype(jnp.bfloat16)
-            send_z[1, at] = jnp.where(first_window, pltpu.roll(even, LANES - WINDOW, axis=1), odd).astype(jnp.bfloat16)
-
-            @pl.when(has_before)
-            def _():
-                side_copy(0, at).start()
-
-            @pl.when(has_after)
-            def _():
-                side_copy(1, at).start()
 
     last = blocks * block - 1
 
@@ -558,37 +553,48 @@
     lax.fori_loop(0, last, stack, 0)
     finish(last, ours(last))
 
-    for at in range(pairs):
+    def hand_on(at, carry):
         @pl.when(has_before)
         def _():
-            side_copy(1, pairs + at).wait_recv()
+            side_copy(1, block + at).wait_recv()
             pass_copy(1, at).start()
 
         @pl.when(has_after)
         def _():
-            side_copy(0, pairs + at).wait_recv()
+            side_copy(0, block + at).wait_recv()
             pass_copy(0, at).start()
 
-    for at in range(pairs):
+        return carry
+
+    lax.fori_loop(0, block, hand_on, 0)
+
+    def assemble(j, carry):
+        epoch_copy(j).wait_recv()
+
         @pl.when(has_before)
         def _():
-            side_copy(1, at).wait_recv()
-            pass_copy(1, at).wait_recv()
+            pass_copy(1, j).wait_recv()
+            side_copy(1, j).wait_recv()
 
         @pl.when(has_after)
         def _():
-            side_copy(0, at).wait_recv()
-            pass_copy(0, at).wait_recv()
-
-        for odd in range(2):
-            j = 2 * at + odd
-            epoch_copy(j).wait_recv()
-            strips_in = jnp.concatenate([recv_z[1, at], recv_z[0, at], passed[1, at], passed[0, at]], axis=1)
-            for m, out in enumerate((psi_out, phi_out)):
-                added = jnp.dot(
-                    strips_in, jnp.concatenate([unplace[odd, m]] * 2, axis=0), preferred_element_type=jnp.float32
+            pass_copy(0, j).wait_recv()
+            side_copy(0, j).wait_recv()
+
+        strips_in = jnp.concatenate([recv_z[1, j], recv_z[0, j], passed[1, j], passed[0, j]], axis=1)
+        for m, out in enumerate((psi_out, phi_out)):
+            added = jnp.dot(
+                strips_in, jnp.concatenate([unplace[m]] * 2, axis=0), preferred_element_type=jnp.float32
+            )
+            for bottom in range(2):
+                span = slice(bottom * tile // 2, (bottom + 1) * tile // 2)
+                out[j, span] = (
+                    keep[j, m, span] + recv_x[j, m, span].astype(jnp.float32)
+                    + added[:, bottom * LANES : (bottom + 1) * LANES]
                 )
-                out[j] = keep[j, m] + recv_x[j, m].astype(jnp.float32) + added
+        return carry
+
+    lax.fori_loop(0, block, assemble, 0)
 
     def drain_v(at, carry):
         vel_copy(at).wait_send()
@@ -602,16 +608,31 @@
 
     lax.fori_loop(0, block, drain_x, 0)
 
-    for to_after, there, back in ((0, has_before, has_after), (1, has_after, has_before)):
-        @pl.when(there)
-        def _():
-            for at in range(blocks * pairs):
-                side_copy(to_after, at).wait_send()
-
-        @pl.when(back)
-        def _():
-            for at in range(pairs):
-                pass_copy(to_after, at).wait_send()
+    def drain_z(at, carry):
+        @pl.when(has_before)
+        def _():
+            side_copy(0, at).wait_send()
+
+        @pl.when(has_after)
+        def _():
+            side_copy(1, at).wait_send()
+
+        return carry
+
+    lax.fori_loop(0, blocks * block, drain_z, 0)
+
+    def drain_passed(at, carry):
+        @pl.when(has_before)
+        def _():
+            pass_copy(1, at).wait_send()
+
+        @pl.when(has_after)
+        def _():
+            pass_copy(0, at).wait_send()
+
+        return carry
+
+    lax.fori_loop(0, block, drain_passed, 0)
 
 
 def near_stacks(images, variances, valid, psf_sigma, offsets, plan):
@@ -622,7 +643,6 @@
     anywhere = pl.BlockSpec(memory_space=pl.ANY)
     dma = pltpu.SemaphoreType.DMA
     half = blocks * block
-    pairs = block // 2
     narrow, wide = jnp.bfloat16, jnp.float32
     scratch = [
         pltpu.VMEM((2 * (epochs + 1) * rows_out, LANES), wide),
@@ -635,7 +655,7 @@
         dma((2, epochs // chunk)),
         pltpu.VMEM((2 * REACH + 1, tile, 2 * LANES), narrow),
         pltpu.VMEM((2 * REACH + 1, EDGE, 2 * LANES), narrow),
-        pltpu.VMEM((2, 2, 2 * tile, LANES), narrow),
+        pltpu.VMEM((2, 2 * tile, 2 * LANES), narrow),
         pltpu.VMEM((rows_out, tile), wide),
         pltpu.VMEM((2 * PACK, LANES), wide),
         pltpu.VMEM((epochs, 2, rows_out, tile), narrow),
@@ -646,24 +666,23 @@
         pltpu.VMEM((block, 2, tile, tile), narrow),
         pltpu.VMEM((block, 2, tile, tile), narrow),
         pltpu.VMEM((block, 2, tile, tile), wide),
-        pltpu.VMEM((half, tile, LANES), wide),
-        pltpu.VMEM((2, half // 2, tile, LANES), narrow),
-        pltpu.VMEM((2, half // 2, tile, LANES), narrow),
-        pltpu.VMEM((2, pairs, tile, LANES), narrow),
+        pltpu.VMEM((2, half, tile // 2, LANES), narrow),
+        pltpu.VMEM((2, half, tile // 2, LANES), narrow),
+        pltpu.VMEM((2, block, tile // 2, LANES), narrow),
         dma((half,)), dma((half,)), dma((block,)), dma((block,)),
-        dma((2, half // 2)), dma((2, half // 2)), dma((2, pairs)), dma((2, pairs)),
+        dma((2, half)), dma((2, half)), dma((2, block)), dma((2, block)),
     ]
     out = jax.ShapeDtypeStruct((block, tile, tile), jnp.float32)
     return pl.pallas_call(
         functools.partial(near_kernel, plan),
         out_shape=(out, out),
-        in_specs=[smem, vmem, smem, smem, anywhere, anywhere],
+        in_specs=[vmem, smem, smem, anywhere, anywhere],
         out_specs=(vmem, vmem),
         scratch_shapes=scratch,
         compiler_params=pltpu.CompilerParams(
             collective_id=0, has_side_effects=True, vmem_limit_bytes=KEPT
         ),
-    )(offsets, offsets, psf_sigma, valid.reshape(epochs), images, variances)
+    )(offsets, psf_sigma, valid.reshape(epochs), images, variances)
 
 
 def far_stacks(images, variances, valid, psf_sigma, offsets, plan):
@@ -718,7 +737,7 @@
     runs = 1 + 2 * -(-REACH * (epochs - 1) // last_epoch)
     plan = (tile, sky, blocks, block, epochs, runs)
     few = EDGE * runs < LANES and epochs % CHUNK == 0
-    if sky == GRID_X and blocks == 2 and lax.axis_size("vel") == 2 and block % 2 == 0 and few:
+    if sky == GRID_X and blocks == 2 and lax.axis_size("vel") == 2 and few:
         plan += (CHUNK,)
         psi_sum, phi_sum = near_stacks(images, variances, valid, psf_sigma, offsets, plan)
     else:

time: 24.8 us -> 23.3 us (0.940)
  Pallas kernels: 21.7 us -> 20.2 us
    pallas_call x1, Pallas kernels: 21.7 us -> 20.2 us  [near_stacks(): pl.pallas_call(functools.partial(near_kernel, plan), out_shape=(out, out)...]
where the time goes in v6:
time: 23.3 us; the launch traced here: 23.1 us
  Pallas kernels  20.2 us (87%)
  local copies, waits for them, and re-layouts  1.37 us (6%)
  other arithmetic  0.87 us (4%)
  between operations  0.66 us (3%)
    pallas_call x1, Pallas kernels, near_stacks(): pl.pallas_call(functools.partial(near_kernel, plan), out_shape=(out, out)...  20.2 us
    unnamed x6, local copies, waits for them, and re-layouts  1.37 us
    unnamed x1, other arithmetic  0.87 us

profile of v6, /device:TPU:0, one launch (start us, length us, event | category | flops | bytes accessed | tf_op | source)
XLA Modules:
  0.0 23.1 jit_solution(11276971076710085717)
XLA Ops:
  0.6 0.0 copy-start.1
  0.6 0.0 copy-start.2
  0.7 0.6 %copy-done.1 = f32[16]{0:T(128)S(1)} copy-done((f32[16]{0:T(128)S(1)}, f32[16]{0:T(128)}, u32[]{:S(2)}) %copy-start.1) | copy-done | bytes 88
  1.3 0.0 copy-done.2
  1.3 0.0 copy-start
  1.3 0.7 %copy-done = s32[2,16,32]{2,1,0:T(8,128)S(1)} copy-done((s32[2,16,32]{2,1,0:T(8,128)S(1)}, s32[2,16,32]{2,1,0:T(8,128)}, u32[]{:S(2)}) %copy-start) | copy-done | bytes 4120
  2.0 20.2 %shard_map.68 = (f32[4,128,128]{2,1,0:T(8,128)S(1)}, f32[4,128,128]{2,1,0:T(8,128)S(1)}) custom-call(s32[2,16,32]{2,1,0:T(8,128)S(1)} %copy-done, f32[16]{0:T(128)S(1)} %copy-done.1, s32[16]{0:T(128)S(1)} %bitcast.9, bf16[16,1,128,128]{3,2,1,0:T(8,128)(2,1)} %refs_3_.1, bf16[16,1,128,128]{3,2,1,0:T(8,128)(2,1)} %refs_4_.1), custom_call_target="tpu_custom_call" | custom-call | tf_op jit(solution)/shard_map/pallas_call | solution.py:676
  22.2 0.9 %divide_bitcast_fusion = (f32[4,1,128,128]{3,2,1,0:T(8,128)}, f32[4,1,128,128]{3,2,1,0:T(8,128)}) fusion(f32[4,128,128]{2,1,0:T(8,128)S(1)} %get-tuple-element.4, f32[4,128,128]{2,1,0:T(8,128)S(1)} %get-tuple-element.5), kind=kLoop, calls=%fused_computation | loop fusion | flops 196608 | bytes 1048576
Async XLA Ops:
  0.6 0.7 %copy-start.1 = (f32[16]{0:T(128)S(1)}, f32[16]{0:T(128)}, u32[]{:S(2)}) copy-start(f32[16]{0:T(128)} %refs_1_.1) | copy-start | bytes 196
  0.6 0.7 %copy-start.2 = (s32[16,1]{0,1:T(1,128)S(1)}, s32[16,1]{0,1:T(1,128)}, u32[]{:S(2)}) copy-start(s32[16,1]{0,1:T(1,128)} %param.7) | copy-start | bytes 196
  1.3 0.7 %copy-start = (s32[2,16,32]{2,1,0:T(8,128)S(1)}, s32[2,16,32]{2,1,0:T(8,128)}, u32[]{:S(2)}) copy-start(s32[2,16,32]{2,1,0:T(8,128)} %refs_0_.1) | copy-start | bytes 12292

commit v7 on v6

--- a/solution.py
+++ b/solution.py
@@ -18,7 +18,6 @@
 EDGE = 16
 WINDOW = 32
 CHUNK = 4
-STEP = 4
 KEPT = 55705600
 
 phi_floor = 0.25
@@ -305,12 +304,14 @@
     short = iota((EDGE, LANES), 1)
     from_edge = edge_column(iota((EDGE, LANES), 0))
 
+    moves = (row - lane, row - beyond(lane), from_edge - short, from_edge - beyond(short))
+
     def make_shift(at, carry):
         right = at - REACH
-        shift[at, :, :LANES] = one_hot(row == lane + right)
-        shift[at, :, LANES:] = one_hot(row == beyond(lane) + right)
-        edge_shift[at, :, :LANES] = one_hot(from_edge == short + right)
-        edge_shift[at, :, LANES:] = one_hot(from_edge == beyond(short) + right)
+        shift[at, :, :LANES] = one_hot(moves[0] == right)
+        shift[at, :, LANES:] = one_hot(moves[1] == right)
+        edge_shift[at, :, :LANES] = one_hot(moves[2] == right)
+        edge_shift[at, :, LANES:] = one_hot(moves[3] == right)
         return carry
 
     lax.fori_loop(0, 2 * REACH + 1, make_shift, 0)
@@ -411,21 +412,29 @@
         ends_at = pl.multiple_of((e + 1) * rows_out, 8)
         edge[pl.ds(ends_at, rows_out)] = edge[pl.ds(begin, rows_out)] + jnp.where(own_half, rims[0], rims[1])
 
-    def all_across(c, carry):
+    def arrive(c):
         for which in range(2):
             load(which, c).wait()
+
+    def all_across(c):
         for turn in range(chunk):
             across(chunk * c + turn)
-        return carry
-
-    lax.fori_loop(0, epochs // chunk, all_across, 0)
-
-    def all_down(c, carry):
-        for turn in range(STEP):
-            down(STEP * c + turn)
-        return carry
-
-    lax.fori_loop(0, epochs // STEP, all_down, 0)
+
+    def all_down(c):
+        for turn in range(chunk):
+            down(chunk * c + turn)
+
+    def both_ways(c, carry):
+        arrive(c)
+        all_down(c - 1)
+        all_across(c)
+        return carry
+
+    chunks = epochs // chunk
+    arrive(0)
+    all_across(0)
+    lax.fori_loop(1, chunks, both_ways, 0)
+    all_down(chunks - 1)
 
     def vel_copy(at):
         return pltpu.make_async_remote_copy(
@@ -568,6 +577,31 @@
 
     lax.fori_loop(0, block, hand_on, 0)
 
+    def drain_v(at, carry):
+        vel_copy(at).wait_send()
+        return carry
+
+    lax.fori_loop(0, blocks * block, drain_v, 0)
+
+    def drain_x(at, carry):
+        epoch_copy(at).wait_send()
+        return carry
+
+    lax.fori_loop(0, block, drain_x, 0)
+
+    def drain_z(at, carry):
+        @pl.when(has_before)
+        def _():
+            side_copy(0, at).wait_send()
+
+        @pl.when(has_after)
+        def _():
+            side_copy(1, at).wait_send()
+
+        return carry
+
+    lax.fori_loop(0, blocks * block, drain_z, 0)
+
     def assemble(j, carry):
         epoch_copy(j).wait_recv()
 
@@ -595,31 +629,6 @@
         return carry
 
     lax.fori_loop(0, block, assemble, 0)
-
-    def drain_v(at, carry):
-        vel_copy(at).wait_send()
-        return carry
-
-    lax.fori_loop(0, blocks * block, drain_v, 0)
-
-    def drain_x(at, carry):
-        epoch_copy(at).wait_send()
-        return carry
-
-    lax.fori_loop(0, block, drain_x, 0)
-
-    def drain_z(at, carry):
-        @pl.when(has_before)
-        def _():
-            side_copy(0, at).wait_send()
-
-        @pl.when(has_after)
-        def _():
-            side_copy(1, at).wait_send()
-
-        return carry
-
-    lax.fori_loop(0, blocks * block, drain_z, 0)
 
     def drain_passed(at, carry):
         @pl.when(has_before)

time: 23.3 us -> 22.6 us (0.970)
  Pallas kernels: 20.2 us -> 19.5 us
    pallas_call x1, Pallas kernels: 20.2 us -> 19.5 us  [near_stacks(): pl.pallas_call(functools.partial(near_kernel, plan), out_shape=(out, out)...]
where the time goes in v7:
time: 22.6 us; the launch traced here: 22.4 us
  Pallas kernels  19.5 us (86%)
  local copies, waits for them, and re-layouts  1.37 us (6%)
  other arithmetic  0.87 us (4%)
  between operations  0.66 us (3%)
    pallas_call x1, Pallas kernels, near_stacks(): pl.pallas_call(functools.partial(near_kernel, plan), out_shape=(out, out)...  19.5 us
    unnamed x6, local copies, waits for them, and re-layouts  1.37 us
    unnamed x1, other arithmetic  0.87 us

profile of v7, /device:TPU:0, one launch (start us, length us, event | category | flops | bytes accessed | tf_op | source)
XLA Modules:
  0.0 22.4 jit_solution(17084684307415617993)
XLA Ops:
  0.6 0.0 copy-start.1
  0.6 0.0 copy-start.2
  0.7 0.6 %copy-done.1 = f32[16]{0:T(128)S(1)} copy-done((f32[16]{0:T(128)S(1)}, f32[16]{0:T(128)}, u32[]{:S(2)}) %copy-start.1) | copy-done | bytes 88
  1.3 0.0 copy-done.2
  1.3 0.0 copy-start
  1.3 0.7 %copy-done = s32[2,16,32]{2,1,0:T(8,128)S(1)} copy-done((s32[2,16,32]{2,1,0:T(8,128)S(1)}, s32[2,16,32]{2,1,0:T(8,128)}, u32[]{:S(2)}) %copy-start) | copy-done | bytes 4120
  2.0 19.5 %shard_map.68 = (f32[4,128,128]{2,1,0:T(8,128)S(1)}, f32[4,128,128]{2,1,0:T(8,128)S(1)}) custom-call(s32[2,16,32]{2,1,0:T(8,128)S(1)} %copy-done, f32[16]{0:T(128)S(1)} %copy-done.1, s32[16]{0:T(128)S(1)} %bitcast.9, bf16[16,1,128,128]{3,2,1,0:T(8,128)(2,1)} %refs_3_.1, bf16[16,1,128,128]{3,2,1,0:T(8,128)(2,1)} %refs_4_.1), custom_call_target="tpu_custom_call" | custom-call | tf_op jit(solution)/shard_map/pallas_call | solution.py:685
  21.5 0.9 %divide_bitcast_fusion = (f32[4,1,128,128]{3,2,1,0:T(8,128)}, f32[4,1,128,128]{3,2,1,0:T(8,128)}) fusion(f32[4,128,128]{2,1,0:T(8,128)S(1)} %get-tuple-element.4, f32[4,128,128]{2,1,0:T(8,128)S(1)} %get-tuple-element.5), kind=kLoop, calls=%fused_computation | loop fusion | flops 196608 | bytes 1048576
Async XLA Ops:
  0.6 0.7 %copy-start.1 = (f32[16]{0:T(128)S(1)}, f32[16]{0:T(128)}, u32[]{:S(2)}) copy-start(f32[16]{0:T(128)} %refs_1_.1) | copy-start | bytes 196
  0.6 0.7 %copy-start.2 = (s32[16,1]{0,1:T(1,128)S(1)}, s32[16,1]{0,1:T(1,128)}, u32[]{:S(2)}) copy-start(s32[16,1]{0,1:T(1,128)} %param.7) | copy-start | bytes 196
  1.3 0.7 %copy-start = (s32[2,16,32]{2,1,0:T(8,128)S(1)}, s32[2,16,32]{2,1,0:T(8,128)}, u32[]{:S(2)}) copy-start(s32[2,16,32]{2,1,0:T(8,128)} %refs_0_.1) | copy-start | bytes 12292

commit v8 on v7

--- a/solution.py
+++ b/solution.py
@@ -282,6 +282,16 @@
         for which in range(2):
             load(which, c).start()
 
+    @pl.when(column == 0)
+    def _():
+        recv_z[1] = jnp.zeros_like(recv_z[1])
+        passed[1] = jnp.zeros_like(passed[1])
+
+    @pl.when(column == GRID_X - 1)
+    def _():
+        recv_z[0] = jnp.zeros_like(recv_z[0])
+        passed[0] = jnp.zeros_like(passed[0])
+
     def iota(shape, axis):
         return lax.broadcasted_iota(jnp.int32, shape, axis)
 
@@ -304,14 +314,17 @@
     short = iota((EDGE, LANES), 1)
     from_edge = edge_column(iota((EDGE, LANES), 0))
 
-    moves = (row - lane, row - beyond(lane), from_edge - short, from_edge - beyond(short))
+    outward = row - beyond(lane)
+    moves = (row - lane, outward[:WINDOW], outward[tile - PACK :], from_edge - short, from_edge - beyond(short))
 
     def make_shift(at, carry):
         right = at - REACH
         shift[at, :, :LANES] = one_hot(moves[0] == right)
-        shift[at, :, LANES:] = one_hot(moves[1] == right)
-        edge_shift[at, :, :LANES] = one_hot(moves[2] == right)
-        edge_shift[at, :, LANES:] = one_hot(moves[3] == right)
+        shift[at, :WINDOW, LANES:] = one_hot(moves[1] == right)
+        shift[at, WINDOW : tile - PACK, LANES:] = jnp.zeros((tile - PACK - WINDOW, LANES), jnp.bfloat16)
+        shift[at, tile - PACK :, LANES:] = one_hot(moves[2] == right)
+        edge_shift[at, :, :LANES] = one_hot(moves[3] == right)
+        edge_shift[at, :, LANES:] = one_hot(moves[4] == right)
         return carry
 
     lax.fori_loop(0, 2 * REACH + 1, make_shift, 0)
@@ -327,6 +340,25 @@
     at = iota(edge_q.shape, 0)
     at = jnp.where(at < PACK, at, at + tile - 2 * PACK)
     edge_q[...] = exponents(at - edge_column(iota(edge_q.shape, 1)))
+
+    def make_bands(e):
+        sigma = jnp.full((8, LANES), sigmas[e], jnp.float32)
+        power = 1.0 / (sigma * sigma)
+        tap = iota((8, LANES), 1) - PSFR
+        norm = jnp.sum(jnp.exp(exponents(tap) * power), axis=1, keepdims=True)
+        scale = (1.0 / norm)[:1]
+        power = power[:1, :1]
+        for q, bands in ((row_q, row_bands), (edge_q, edge_bands)):
+            profile = jnp.exp(q[...] * power) * scale
+            bands[e, 0] = profile.astype(jnp.bfloat16)
+            bands[e, 1] = (profile * profile).astype(jnp.bfloat16)
+
+    def all_bands(c, carry):
+        for turn in range(chunk):
+            make_bands(chunk * c + turn)
+        return carry
+
+    all_bands(0, 0)
 
     first = member * epochs
     at_epoch = iota(motion.shape[1:], 1)
@@ -358,34 +390,7 @@
     plane[: maps * rows_out] = jnp.zeros((maps * rows_out, LANES), jnp.float32)
     edge[:rows_out] = jnp.zeros((rows_out, LANES), jnp.float32)
 
-    @pl.when(column == 0)
-    def _():
-        recv_z[1] = jnp.zeros_like(recv_z[1])
-        passed[1] = jnp.zeros_like(passed[1])
-
-    @pl.when(column == GRID_X - 1)
-    def _():
-        recv_z[0] = jnp.zeros_like(recv_z[0])
-        passed[0] = jnp.zeros_like(passed[0])
-
-    def make_bands(e):
-        sigma = jnp.full((8, LANES), sigmas[e], jnp.float32)
-        power = 1.0 / (sigma * sigma)
-        tap = iota((8, LANES), 1) - PSFR
-        norm = jnp.sum(jnp.exp(exponents(tap) * power), axis=1, keepdims=True)
-        scale = (1.0 / norm)[:1]
-        power = power[:1, :1]
-        for q, bands in ((row_q, row_bands), (edge_q, edge_bands)):
-            profile = jnp.exp(q[...] * power) * scale
-            bands[e, 0] = profile.astype(jnp.bfloat16)
-            bands[e, 1] = (profile * profile).astype(jnp.bfloat16)
-
-    def all_bands(c, carry):
-        for turn in range(chunk):
-            make_bands(chunk * c + turn)
-        return carry
-
-    lax.fori_loop(0, epochs // chunk, all_bands, 0)
+    lax.fori_loop(1, epochs // chunk, all_bands, 0)
 
     def across(e):
         usable = valid[e].astype(jnp.float32)
@@ -438,27 +443,27 @@
 
     def vel_copy(at):
         return pltpu.make_async_remote_copy(
-            src_ref=send_v.at[at], dst_ref=recv_v.at[at], send_sem=sv.at[at], recv_sem=rv.at[at],
+            src_ref=send_v.at[at], dst_ref=recv_v.at[at], send_sem=sv, recv_sem=rv.at[at],
             device_id={"vel": partner}, device_id_type=mesh_id,
         )
 
     def epoch_copy(at):
         return pltpu.make_async_remote_copy(
-            src_ref=send_x.at[at], dst_ref=recv_x.at[at], send_sem=sx.at[at], recv_sem=rx.at[at],
+            src_ref=send_x.at[at], dst_ref=recv_x.at[at], send_sem=sx, recv_sem=rx.at[at],
             device_id={"epoch": peer}, device_id_type=mesh_id,
         )
 
     def side_copy(to_after, at):
         return pltpu.make_async_remote_copy(
             src_ref=send_z.at[to_after, at], dst_ref=recv_z.at[to_after, at],
-            send_sem=sz.at[to_after, at], recv_sem=rz.at[to_after, at],
+            send_sem=sz.at[to_after], recv_sem=rz.at[to_after, at],
             device_id={"sky": after if to_after else before}, device_id_type=mesh_id,
         )
 
     def pass_copy(to_after, at):
         return pltpu.make_async_remote_copy(
             src_ref=recv_z.at[to_after, block + at], dst_ref=passed.at[to_after, at],
-            send_sem=sp.at[to_after, at], recv_sem=rp.at[to_after, at],
+            send_sem=sp.at[to_after], recv_sem=rp.at[to_after, at],
             device_id={"epoch": peer}, device_id_type=mesh_id,
         )
 
@@ -577,30 +582,36 @@
 
     lax.fori_loop(0, block, hand_on, 0)
 
-    def drain_v(at, carry):
-        vel_copy(at).wait_send()
-        return carry
-
-    lax.fori_loop(0, blocks * block, drain_v, 0)
-
-    def drain_x(at, carry):
-        epoch_copy(at).wait_send()
-        return carry
-
-    lax.fori_loop(0, block, drain_x, 0)
-
-    def drain_z(at, carry):
-        @pl.when(has_before)
-        def _():
-            side_copy(0, at).wait_send()
-
-        @pl.when(has_after)
-        def _():
-            side_copy(1, at).wait_send()
-
-        return carry
-
-    lax.fori_loop(0, blocks * block, drain_z, 0)
+    pltpu.make_async_remote_copy(
+        src_ref=send_v, dst_ref=recv_v, send_sem=sv, recv_sem=rv.at[0],
+        device_id={"vel": partner}, device_id_type=mesh_id,
+    ).wait_send()
+    pltpu.make_async_remote_copy(
+        src_ref=send_x, dst_ref=recv_x, send_sem=sx, recv_sem=rx.at[0],
+        device_id={"epoch": peer}, device_id_type=mesh_id,
+    ).wait_send()
+
+    def sent_side(to_after):
+        pltpu.make_async_remote_copy(
+            src_ref=send_z.at[to_after], dst_ref=recv_z.at[to_after],
+            send_sem=sz.at[to_after], recv_sem=rz.at[to_after, 0],
+            device_id={"sky": after if to_after else before}, device_id_type=mesh_id,
+        ).wait_send()
+
+    def sent_on(to_after):
+        pltpu.make_async_remote_copy(
+            src_ref=recv_z.at[to_after, pl.ds(block, block)], dst_ref=passed.at[to_after],
+            send_sem=sp.at[to_after], recv_sem=rp.at[to_after, 0],
+            device_id={"epoch": peer}, device_id_type=mesh_id,
+        ).wait_send()
+
+    @pl.when(has_before)
+    def _():
+        sent_side(0)
+
+    @pl.when(has_after)
+    def _():
+        sent_side(1)
 
     def assemble(j, carry):
         epoch_copy(j).wait_recv()
@@ -630,18 +641,13 @@
 
     lax.fori_loop(0, block, assemble, 0)
 
-    def drain_passed(at, carry):
-        @pl.when(has_before)
-        def _():
-            pass_copy(1, at).wait_send()
-
-        @pl.when(has_after)
-        def _():
-            pass_copy(0, at).wait_send()
-
-        return carry
-
-    lax.fori_loop(0, block, drain_passed, 0)
+    @pl.when(has_before)
+    def _():
+        sent_on(1)
+
+    @pl.when(has_after)
+    def _():
+        sent_on(0)
 
 
 def near_stacks(images, variances, valid, psf_sigma, offsets, plan):
@@ -678,8 +684,8 @@
         pltpu.VMEM((2, half, tile // 2, LANES), narrow),
         pltpu.VMEM((2, half, tile // 2, LANES), narrow),
         pltpu.VMEM((2, block, tile // 2, LANES), narrow),
-        dma((half,)), dma((half,)), dma((block,)), dma((block,)),
-        dma((2, half)), dma((2, half)), dma((2, block)), dma((2, block)),
+        dma(()), dma((half,)), dma(()), dma((block,)),
+        dma((2,)), dma((2, half)), dma((2,)), dma((2, block)),
     ]
     out = jax.ShapeDtypeStruct((block, tile, tile), jnp.float32)
     return pl.pallas_call(

time: 22.6 us -> 22 us (0.973)
  Pallas kernels: 19.5 us -> 18.9 us
    pallas_call x1, Pallas kernels: 19.5 us -> 18.9 us  [near_stacks(): pl.pallas_call(functools.partial(near_kernel, plan), out_shape=(out, out)...]
where the time goes in v8:
time: 22 us; the launch traced here: 21.8 us
  Pallas kernels  18.9 us (86%)
  local copies, waits for them, and re-layouts  1.37 us (6%)
  other arithmetic  0.87 us (4%)
  between operations  0.66 us (3%)
    pallas_call x1, Pallas kernels, near_stacks(): pl.pallas_call(functools.partial(near_kernel, plan), out_shape=(out, out)...  18.9 us
    unnamed x6, local copies, waits for them, and re-layouts  1.37 us
    unnamed x1, other arithmetic  0.87 us

profile of v8, /device:TPU:0, one launch (start us, length us, event | category | flops | bytes accessed | tf_op | source)
XLA Modules:
  0.0 21.8 jit_solution(2265914252433778840)
XLA Ops:
  0.6 0.0 copy-start.1
  0.6 0.0 copy-start.2
  0.7 0.6 %copy-done.1 = f32[16]{0:T(128)S(1)} copy-done((f32[16]{0:T(128)S(1)}, f32[16]{0:T(128)}, u32[]{:S(2)}) %copy-start.1) | copy-done | bytes 88
  1.3 0.0 copy-done.2
  1.3 0.0 copy-start
  1.3 0.7 %copy-done = s32[2,16,32]{2,1,0:T(8,128)S(1)} copy-done((s32[2,16,32]{2,1,0:T(8,128)S(1)}, s32[2,16,32]{2,1,0:T(8,128)}, u32[]{:S(2)}) %copy-start) | copy-done | bytes 4120
  2.0 18.9 %shard_map.68 = (f32[4,128,128]{2,1,0:T(8,128)S(1)}, f32[4,128,128]{2,1,0:T(8,128)S(1)}) custom-call(s32[2,16,32]{2,1,0:T(8,128)S(1)} %copy-done, f32[16]{0:T(128)S(1)} %copy-done.1, s32[16]{0:T(128)S(1)} %bitcast.9, bf16[16,1,128,128]{3,2,1,0:T(8,128)(2,1)} %refs_3_.1, bf16[16,1,128,128]{3,2,1,0:T(8,128)(2,1)} %refs_4_.1), custom_call_target="tpu_custom_call" | custom-call | tf_op jit(solution)/shard_map/pallas_call | solution.py:691
  21.0 0.9 %divide_bitcast_fusion = (f32[4,1,128,128]{3,2,1,0:T(8,128)}, f32[4,1,128,128]{3,2,1,0:T(8,128)}) fusion(f32[4,128,128]{2,1,0:T(8,128)S(1)} %get-tuple-element.4, f32[4,128,128]{2,1,0:T(8,128)S(1)} %get-tuple-element.5), kind=kLoop, calls=%fused_computation | loop fusion | flops 196608 | bytes 1048576
Async XLA Ops:
  0.6 0.7 %copy-start.1 = (f32[16]{0:T(128)S(1)}, f32[16]{0:T(128)}, u32[]{:S(2)}) copy-start(f32[16]{0:T(128)} %refs_1_.1) | copy-start | bytes 196
  0.6 0.7 %copy-start.2 = (s32[16,1]{0,1:T(1,128)S(1)}, s32[16,1]{0,1:T(1,128)}, u32[]{:S(2)}) copy-start(s32[16,1]{0,1:T(1,128)} %param.7) | copy-start | bytes 196
  1.3 0.7 %copy-start = (s32[2,16,32]{2,1,0:T(8,128)S(1)}, s32[2,16,32]{2,1,0:T(8,128)}, u32[]{:S(2)}) copy-start(s32[2,16,32]{2,1,0:T(8,128)} %refs_0_.1) | copy-start | bytes 12292

commit v9 on v8

--- a/solution.py
+++ b/solution.py
@@ -390,8 +390,6 @@
     plane[: maps * rows_out] = jnp.zeros((maps * rows_out, LANES), jnp.float32)
     edge[:rows_out] = jnp.zeros((rows_out, LANES), jnp.float32)
 
-    lax.fori_loop(1, epochs // chunk, all_bands, 0)
-
     def across(e):
         usable = valid[e].astype(jnp.float32)
         inverse = usable / variance[e].astype(jnp.float32)
@@ -433,12 +431,16 @@
         arrive(c)
         all_down(c - 1)
         all_across(c)
-        return carry
+        return all_bands(c + 1, carry)
 
     chunks = epochs // chunk
     arrive(0)
     all_across(0)
-    lax.fori_loop(1, chunks, both_ways, 0)
+    all_bands(1, 0)
+    lax.fori_loop(1, chunks - 1, both_ways, 0)
+    arrive(chunks - 1)
+    all_down(chunks - 2)
+    all_across(chunks - 1)
     all_down(chunks - 1)
 
     def vel_copy(at):
@@ -751,7 +753,7 @@
     last_epoch = epochs * blocks * lax.axis_size("vel") - 1
     runs = 1 + 2 * -(-REACH * (epochs - 1) // last_epoch)
     plan = (tile, sky, blocks, block, epochs, runs)
-    few = EDGE * runs < LANES and epochs % CHUNK == 0
+    few = EDGE * runs < LANES and epochs % CHUNK == 0 and epochs >= 2 * CHUNK
     if sky == GRID_X and blocks == 2 and lax.axis_size("vel") == 2 and few:
         plan += (CHUNK,)
         psi_sum, phi_sum = near_stacks(images, variances, valid, psf_sigma, offsets, plan)

time: 22 us -> 22 us (level)
  no operation moved by 1% of the time
where the time goes in v9:
time: 22 us; the launch traced here: 21.7 us
  Pallas kernels  18.8 us (85%)
  local copies, waits for them, and re-layouts  1.37 us (6%)
  other arithmetic  0.87 us (4%)
  between operations  0.66 us (3%)
    pallas_call x1, Pallas kernels, near_stacks(): pl.pallas_call(functools.partial(near_kernel, plan), out_shape=(out, out)...  18.8 us
    unnamed x6, local copies, waits for them, and re-layouts  1.37 us
    unnamed x1, other arithmetic  0.87 us

profile of v9, /device:TPU:0, one launch (start us, length us, event | category | flops | bytes accessed | tf_op | source)
XLA Modules:
  0.0 21.7 jit_solution(10856121024293220915)
XLA Ops:
  0.6 0.0 copy-start.1
  0.6 0.0 copy-start.2
  0.7 0.6 %copy-done.1 = f32[16]{0:T(128)S(1)} copy-done((f32[16]{0:T(128)S(1)}, f32[16]{0:T(128)}, u32[]{:S(2)}) %copy-start.1) | copy-done | bytes 88
  1.3 0.0 copy-done.2
  1.3 0.0 copy-start
  1.3 0.7 %copy-done = s32[2,16,32]{2,1,0:T(8,128)S(1)} copy-done((s32[2,16,32]{2,1,0:T(8,128)S(1)}, s32[2,16,32]{2,1,0:T(8,128)}, u32[]{:S(2)}) %copy-start) | copy-done | bytes 4120
  2.0 18.8 %shard_map.68 = (f32[4,128,128]{2,1,0:T(8,128)S(1)}, f32[4,128,128]{2,1,0:T(8,128)S(1)}) custom-call(s32[2,16,32]{2,1,0:T(8,128)S(1)} %copy-done, f32[16]{0:T(128)S(1)} %copy-done.1, s32[16]{0:T(128)S(1)} %bitcast.9, bf16[16,1,128,128]{3,2,1,0:T(8,128)(2,1)} %refs_3_.1, bf16[16,1,128,128]{3,2,1,0:T(8,128)(2,1)} %refs_4_.1), custom_call_target="tpu_custom_call" | custom-call | tf_op jit(solution)/shard_map/pallas_call | solution.py:693
  20.9 0.9 %divide_bitcast_fusion = (f32[4,1,128,128]{3,2,1,0:T(8,128)}, f32[4,1,128,128]{3,2,1,0:T(8,128)}) fusion(f32[4,128,128]{2,1,0:T(8,128)S(1)} %get-tuple-element.4, f32[4,128,128]{2,1,0:T(8,128)S(1)} %get-tuple-element.5), kind=kLoop, calls=%fused_computation | loop fusion | flops 196608 | bytes 1048576
Async XLA Ops:
  0.6 0.7 %copy-start.1 = (f32[16]{0:T(128)S(1)}, f32[16]{0:T(128)}, u32[]{:S(2)}) copy-start(f32[16]{0:T(128)} %refs_1_.1) | copy-start | bytes 196
  0.6 0.7 %copy-start.2 = (s32[16,1]{0,1:T(1,128)S(1)}, s32[16,1]{0,1:T(1,128)}, u32[]{:S(2)}) copy-start(s32[16,1]{0,1:T(1,128)} %param.7) | copy-start | bytes 196
  1.3 0.7 %copy-start = (s32[2,16,32]{2,1,0:T(8,128)S(1)}, s32[2,16,32]{2,1,0:T(8,128)}, u32[]{:S(2)}) copy-start(s32[2,16,32]{2,1,0:T(8,128)} %refs_0_.1) | copy-start | bytes 12292

commit v10 on v8

--- a/solution.py
+++ b/solution.py
@@ -505,16 +505,18 @@
         return summed[:tile, :LANES], summed[tile:, :LANES], outer
 
     def spot_of(turn):
-        return (blocks - 1 - turn // block) * block + lax.rem(turn, block)
+        late = turn == 2 * block - 1
+        near = ((turn > 0) & (lax.rem(turn, 2) == 0)) | late
+        return jnp.where(late, block - 1, jnp.where(near, turn // 2 - 1, block + (turn + 1) // 2))
 
     def owner_of(turn):
         return lax.rem(group + spot_of(turn) // block, blocks) * 2
 
     def theirs(turn):
-        return stacked((owner_of(turn) + partner) * block + lax.rem(turn, block))
+        return stacked((owner_of(turn) + partner) * block + lax.rem(spot_of(turn), block))
 
     def ours(turn):
-        return stacked((owner_of(turn) + member) * block + lax.rem(turn, block))
+        return stacked((owner_of(turn) + member) * block + lax.rem(spot_of(turn), block))
 
     def hand_over(turn, parts):
         spot = spot_of(turn)
@@ -524,7 +526,7 @@
 
     def finish(turn, parts):
         spot = spot_of(turn)
-        j = lax.rem(turn, block)
+        j = lax.rem(spot_of(turn), block)
         vel_copy(spot).wait_recv()
         totals = [parts[m] + recv_v[spot, m].astype(jnp.float32) for m in range(maps + 1)]
         upper, lower = totals[maps][: tile // 2], totals[maps][tile // 2 :]

time: 22 us -> 23.7 us (1.077)
  Pallas kernels: 18.9 us -> 20.6 us
    pallas_call x1, Pallas kernels: 18.9 us -> 20.6 us  [near_stacks(): pl.pallas_call(functools.partial(near_kernel, plan), out_shape=(out, out)...]
where the time goes in v10:
time: 23.7 us; the launch traced here: 23.5 us
  Pallas kernels  20.6 us (87%)
  local copies, waits for them, and re-layouts  1.37 us (6%)
  other arithmetic  0.87 us (4%)
  between operations  0.66 us (3%)
    pallas_call x1, Pallas kernels, near_stacks(): pl.pallas_call(functools.partial(near_kernel, plan), out_shape=(out, out)...  20.6 us
    unnamed x6, local copies, waits for them, and re-layouts  1.37 us
    unnamed x1, other arithmetic  0.87 us

profile of v10, /device:TPU:0, one launch (start us, length us, event | category | flops | bytes accessed | tf_op | source)
XLA Modules:
  0.0 23.5 jit_solution(16738775209270690468)
XLA Ops:
  0.6 0.0 copy-start.1
  0.6 0.0 copy-start.2
  0.7 0.6 %copy-done.1 = f32[16]{0:T(128)S(1)} copy-done((f32[16]{0:T(128)S(1)}, f32[16]{0:T(128)}, u32[]{:S(2)}) %copy-start.1) | copy-done | bytes 88
  1.3 0.0 copy-done.2
  1.3 0.0 copy-start
  1.3 0.7 %copy-done = s32[2,16,32]{2,1,0:T(8,128)S(1)} copy-done((s32[2,16,32]{2,1,0:T(8,128)S(1)}, s32[2,16,32]{2,1,0:T(8,128)}, u32[]{:S(2)}) %copy-start) | copy-done | bytes 4120
  2.0 20.6 %shard_map.68 = (f32[4,128,128]{2,1,0:T(8,128)S(1)}, f32[4,128,128]{2,1,0:T(8,128)S(1)}) custom-call(s32[2,16,32]{2,1,0:T(8,128)S(1)} %copy-done, f32[16]{0:T(128)S(1)} %copy-done.1, s32[16]{0:T(128)S(1)} %bitcast.9, bf16[16,1,128,128]{3,2,1,0:T(8,128)(2,1)} %refs_3_.1, bf16[16,1,128,128]{3,2,1,0:T(8,128)(2,1)} %refs_4_.1), custom_call_target="tpu_custom_call" | custom-call | tf_op jit(solution)/shard_map/pallas_call | solution.py:693
  22.6 0.9 %divide_bitcast_fusion = (f32[4,1,128,128]{3,2,1,0:T(8,128)}, f32[4,1,128,128]{3,2,1,0:T(8,128)}) fusion(f32[4,128,128]{2,1,0:T(8,128)S(1)} %get-tuple-element.4, f32[4,128,128]{2,1,0:T(8,128)S(1)} %get-tuple-element.5), kind=kLoop, calls=%fused_computation | loop fusion | flops 196608 | bytes 1048576
Async XLA Ops:
  0.6 0.7 %copy-start.1 = (f32[16]{0:T(128)S(1)}, f32[16]{0:T(128)}, u32[]{:S(2)}) copy-start(f32[16]{0:T(128)} %refs_1_.1) | copy-start | bytes 196
  0.6 0.7 %copy-start.2 = (s32[16,1]{0,1:T(1,128)S(1)}, s32[16,1]{0,1:T(1,128)}, u32[]{:S(2)}) copy-start(s32[16,1]{0,1:T(1,128)} %param.7) | copy-start | bytes 196
  1.3 0.7 %copy-start = (s32[2,16,32]{2,1,0:T(8,128)S(1)}, s32[2,16,32]{2,1,0:T(8,128)}, u32[]{:S(2)}) copy-start(s32[2,16,32]{2,1,0:T(8,128)} %refs_0_.1) | copy-start | bytes 12292

commit v11 on v8

--- a/solution.py
+++ b/solution.py
@@ -567,20 +567,36 @@
     lax.fori_loop(0, last, stack, 0)
     finish(last, ours(last))
 
-    def hand_on(at, carry):
-        @pl.when(has_before)
-        def _():
-            side_copy(1, block + at).wait_recv()
-            pass_copy(1, at).start()
-
-        @pl.when(has_after)
-        def _():
-            side_copy(0, block + at).wait_recv()
-            pass_copy(0, at).start()
-
-        return carry
-
-    lax.fori_loop(0, block, hand_on, 0)
+    def hand_on(to_after, at):
+        side_copy(to_after, block + at).wait_recv()
+        pass_copy(to_after, at).start()
+
+    wrapped = column == GRID_X // 2
+
+    def hand_on_near(at, carry):
+        @pl.when(has_before & (column != GRID_X // 2))
+        def _():
+            hand_on(1, at)
+
+        @pl.when(wrapped)
+        def _():
+            hand_on(0, at)
+
+        return carry
+
+    def hand_on_far(at, carry):
+        @pl.when(wrapped)
+        def _():
+            hand_on(1, at)
+
+        @pl.when(has_after & (column != GRID_X // 2))
+        def _():
+            hand_on(0, at)
+
+        return carry
+
+    lax.fori_loop(0, block, hand_on_near, 0)
+    lax.fori_loop(0, block, hand_on_far, 0)
 
     pltpu.make_async_remote_copy(
         src_ref=send_v, dst_ref=recv_v, send_sem=sv, recv_sem=rv.at[0],

time: 22 us -> 22.1 us (level)
  no operation moved by 1% of the time
where the time goes in v11:
time: 22.1 us; the launch traced here: 21.9 us
  Pallas kernels  19 us (86%)
  local copies, waits for them, and re-layouts  1.37 us (6%)
  other arithmetic  0.87 us (4%)
  between operations  0.66 us (3%)
    pallas_call x1, Pallas kernels, near_stacks(): pl.pallas_call(functools.partial(near_kernel, plan), out_shape=(out, out)...  19 us
    unnamed x6, local copies, waits for them, and re-layouts  1.37 us
    unnamed x1, other arithmetic  0.87 us

profile of v11, /device:TPU:0, one launch (start us, length us, event | category | flops | bytes accessed | tf_op | source)
XLA Modules:
  0.0 21.9 jit_solution(15637314157699586088)
XLA Ops:
  0.6 0.0 copy-start.1
  0.6 0.0 copy-start.2
  0.7 0.6 %copy-done.1 = f32[16]{0:T(128)S(1)} copy-done((f32[16]{0:T(128)S(1)}, f32[16]{0:T(128)}, u32[]{:S(2)}) %copy-start.1) | copy-done | bytes 88
  1.3 0.0 copy-done.2
  1.3 0.0 copy-start
  1.3 0.7 %copy-done = s32[2,16,32]{2,1,0:T(8,128)S(1)} copy-done((s32[2,16,32]{2,1,0:T(8,128)S(1)}, s32[2,16,32]{2,1,0:T(8,128)}, u32[]{:S(2)}) %copy-start) | copy-done | bytes 4120
  2.0 19.0 %shard_map.68 = (f32[4,128,128]{2,1,0:T(8,128)S(1)}, f32[4,128,128]{2,1,0:T(8,128)S(1)}) custom-call(s32[2,16,32]{2,1,0:T(8,128)S(1)} %copy-done, f32[16]{0:T(128)S(1)} %copy-done.1, s32[16]{0:T(128)S(1)} %bitcast.9, bf16[16,1,128,128]{3,2,1,0:T(8,128)(2,1)} %refs_3_.1, bf16[16,1,128,128]{3,2,1,0:T(8,128)(2,1)} %refs_4_.1), custom_call_target="tpu_custom_call" | custom-call | tf_op jit(solution)/shard_map/pallas_call | solution.py:707
  21.0 0.9 %divide_bitcast_fusion = (f32[4,1,128,128]{3,2,1,0:T(8,128)}, f32[4,1,128,128]{3,2,1,0:T(8,128)}) fusion(f32[4,128,128]{2,1,0:T(8,128)S(1)} %get-tuple-element.4, f32[4,128,128]{2,1,0:T(8,128)S(1)} %get-tuple-element.5), kind=kLoop, calls=%fused_computation | loop fusion | flops 196608 | bytes 1048576
Async XLA Ops:
  0.6 0.7 %copy-start.1 = (f32[16]{0:T(128)S(1)}, f32[16]{0:T(128)}, u32[]{:S(2)}) copy-start(f32[16]{0:T(128)} %refs_1_.1) | copy-start | bytes 196
  0.6 0.7 %copy-start.2 = (s32[16,1]{0,1:T(1,128)S(1)}, s32[16,1]{0,1:T(1,128)}, u32[]{:S(2)}) copy-start(s32[16,1]{0,1:T(1,128)} %param.7) | copy-start | bytes 196
  1.3 0.7 %copy-start = (s32[2,16,32]{2,1,0:T(8,128)S(1)}, s32[2,16,32]{2,1,0:T(8,128)}, u32[]{:S(2)}) copy-start(s32[2,16,32]{2,1,0:T(8,128)} %refs_0_.1) | copy-start | bytes 12292
